TPU v7x, 256 devices: a whole 4x4x8 slice. The times are simulated.
256 devices in a mesh: rep: 4 (over x_lo, core), fsdp: 64 (over z, x_hi, y).
Axes of the slice: x: 4 (x_hi: 2, x_lo: 2; x = x_hi * 2 + x_lo), y: 4, z: 8, core: 2. Of those that a mesh axis runs over, the one named last changes fastest.
Arguments:
- tokens: bfloat16 [4096, 4096], P(('rep', 'fsdp')), may hold values from -6 to 6
- readout: bfloat16 [4096, 14336], P('rep', 'fsdp'), may hold values from -0.046875 to 0.046875
- resp_mask: int32 [4096], P('rep'), may hold values 0 or 1
- order: int32 [4, 64], P('rep'), may hold values from 0 to 63, each once within a row
- w_gate: bfloat16 [4, 14336, 4096], P('rep', 'fsdp'), may hold values from -0.09375 to 0.09375
- w_up: bfloat16 [4, 14336, 4096], P('rep', 'fsdp'), may hold values from -0.09375 to 0.09375
- outer_gate: bfloat16 [14336, 4096], P('fsdp', 'rep'), may hold values from -0.09375 to 0.09375
- outer_up: bfloat16 [14336, 4096], P('fsdp', 'rep'), may hold values from -0.09375 to 0.09375
- moment: float32 [14336, 4096], P('fsdp', 'rep'), may hold values from -0.09375 to 0.09375
Outputs:
- loss: float32 [4], P('rep')
- grad_gate: bfloat16 [4, 14336, 4096], P('rep', 'fsdp')
- grad_up: bfloat16 [4, 14336, 4096], P('rep', 'fsdp')
- new_outer: bfloat16 [14336, 4096], P('fsdp', 'rep')
- new_moment: float32 [14336, 4096], P('fsdp', 'rep')
Inputs may be any that keep to these rules, and one draw needn't show every extreme that they name: Each row of order holds every sequence number of its group once.
All inputs are finite; a program needn't handle non-finite values. Where the computation divides by a largest or mean magnitude, that divisor is 1e-20 or more. No bound on the sum of `resp_mask` on one device may be relied on, other than what follows from the above.
Results may differ from a plain program's by a relative error of at most 0.022.
Values may be sent and summed in bfloat16 or wider, within the bound.
A program may use at most 128 MiB of HBM per device.

v0:
```python
import jax
import jax.numpy as jnp
from jax import lax
from jax.sharding import PartitionSpec as P

BLOCK = 128
LEN = 16


dpo_beta = 0.1
outer_rate = 0.7
outer_mu = 0.9
tiny_eps = 1e-06


def project(rows, weight):
    return lax.dot_general(
        rows, weight, (((1,), (1,)), ((), ())), preferred_element_type=jnp.float32
    )


def local_scores(hidden, readout, mask_f, seqs):
    per_token = jnp.sum(hidden.astype(jnp.float32) * readout.astype(jnp.float32), axis=1)
    return jnp.sum((per_token * mask_f).reshape(seqs, LEN), axis=1)


def per_device(tokens, readout, resp_mask, order, w_gate, w_up, outer_gate, outer_up, moment):
    full_gate, full_up = (
        lax.all_gather(outer_gate, "rep", axis=1, tiled=True),
        lax.all_gather(outer_up, "rep", axis=1, tiled=True),
    )
    policy_gate = w_gate[0]
    policy_up = w_up[0]
    inputs = lax.all_gather(tokens, "fsdp", axis=0, tiled=True)
    gate = project(inputs, policy_gate)
    upper = project(inputs, policy_up)
    gate_ref = project(inputs, full_gate)
    upper_ref = project(inputs, full_up)
    group_tok = inputs.shape[0]
    seqs = group_tok // LEN
    mask_f = resp_mask.astype(jnp.float32)
    hidden = (jax.nn.silu(gate) * upper).astype(jnp.bfloat16)
    hidden_ref = (jax.nn.silu(gate_ref) * upper_ref).astype(jnp.bfloat16)
    score, score_ref = lax.psum(
        (
            local_scores(hidden, readout, mask_f, seqs),
            local_scores(hidden_ref, readout, mask_f, seqs),
        ),
        "fsdp",
    )
    places = jnp.arange(seqs, dtype=jnp.int32)
    pick_chosen = (order[0, 0::2][:, None] == places[None, :]).astype(jnp.float32)
    pick_rejected = (order[0, 1::2][:, None] == places[None, :]).astype(jnp.float32)
    relative = score - score_ref
    highest = lax.Precision.HIGHEST
    margin = dpo_beta * (
        jnp.dot(pick_chosen, relative, precision=highest)
        - jnp.dot(pick_rejected, relative, precision=highest)
    )
    loss = jnp.mean(jax.nn.softplus(-margin)).reshape(1)
    weight = dpo_beta * jax.nn.sigmoid(-margin) / pick_chosen.shape[0]
    coef = jnp.dot(weight, pick_rejected - pick_chosen, precision=highest)
    token_grad = jnp.broadcast_to(coef[:, None], (seqs, LEN)).reshape(-1) * mask_f
    hidden_grad = token_grad[:, None] * readout.astype(jnp.float32)
    sigma = jax.nn.sigmoid(gate)
    gate_grad = (hidden_grad * upper * sigma * (1.0 + gate * (1.0 - sigma))).astype(jnp.bfloat16)
    up_grad = (hidden_grad * jax.nn.silu(gate)).astype(jnp.bfloat16)
    contract = (((0,), (0,)), ((), ()))
    grad_gate = lax.dot_general(
        gate_grad, inputs, contract, preferred_element_type=jnp.float32
    ).astype(jnp.bfloat16)
    grad_up = lax.dot_general(up_grad, inputs, contract, preferred_element_type=jnp.float32).astype(
        jnp.bfloat16
    )
    unit_rows = full_gate.shape[0]
    delta = full_gate.astype(jnp.float32) - policy_gate.astype(jnp.float32)
    blocks = delta.reshape(unit_rows, -1, BLOCK)
    scale = (jnp.max(jnp.abs(blocks), axis=2, keepdims=True) + tiny_eps).astype(jnp.bfloat16)
    levels = (blocks / scale.astype(jnp.float32)).astype(jnp.bfloat16)
    groups = lax.axis_size("rep")
    terms = (levels.astype(jnp.float32) * scale.astype(jnp.float32)).reshape(unit_rows, -1)
    total = lax.psum_scatter(
        terms.astype(jnp.bfloat16), "rep", scatter_dimension=1, tiled=True
    ).astype(jnp.float32)
    average = total / groups
    new_moment = outer_mu * moment + average
    new_outer = (
        outer_gate.astype(jnp.float32) - outer_rate * (average + outer_mu * new_moment)
    ).astype(jnp.bfloat16)
    return (loss, grad_gate[None], grad_up[None], new_outer, new_moment)


def solution(mesh):
    return jax.shard_map(
        per_device,
        mesh=mesh,
        in_specs=(
            P(("rep", "fsdp"), None),
            P("rep", "fsdp"),
            P("rep"),
            P("rep", None),
            P("rep", "fsdp", None),
            P("rep", "fsdp", None),
            P("fsdp", "rep"),
            P("fsdp", "rep"),
            P("fsdp", "rep"),
        ),
        out_specs=(
            P("rep"),
            P("rep", "fsdp", None),
            P("rep", "fsdp", None),
            P("fsdp", "rep"),
            P("fsdp", "rep"),
        ),
        check_vma=False,
    )
```

profile of v0, /device:TPU:2, one launch (start us, length us, event | category | flops | bytes accessed | tf_op | source)
XLA Modules:
  0.0 466.0 jit_solution(16427178451897451544)
XLA Ops:
  8.1 0.7 all-gather.6.cloned.1.call-update
  8.8 32.6 %all-gather.6.cloned.1.call-done = bf16[224,4096]{1,0:T(8,128)(2,1)} async-done(((bf16[224,1024]{1,0:T(8,128)(2,1)}), bf16[224,4096]{1,0:T(8,128)(2,1)}) %all-gather.6.cloned.1.call-update) | async-done | bytes 1835024 | tf_op jit(solution)/shard_map/all_gather | solution.py:29
  41.4 2.7 abs_bitcast_fusion
  44.2 2.4 copy.14
  46.6 3.1 reduce_max.9
  49.7 1.0 div.44
  50.7 0.5 copy-done.1
  51.2 0.6 copy-done.2
  51.7 4.3 fusion.3
  56.1 0.5 all-gather.4.cloned.1.call-update
  56.7 0.2 all-gather.8.cloned.1.call-start
  56.9 0.4 all-gather.8.cloned.1.call-update
  57.5 29.5 %reduce-scatter.2.cloned.1.call-done = bf16[224,1024]{1,0:T(8,128)(2,1)} async-done(((bf16[224,4096]{1,0:T(8,128)(2,1)}), bf16[224,1024]{1,0:T(8,128)(2,1)}) %reduce-scatter.2.cloned.1.call-update) | async-done | bytes 458768 | tf_op jit(solution)/shard_map/reduce_scatter | solution.py:82
  87.0 2.4 subtract_convert_fusion
  89.4 125.4 %all-gather.4.cloned.1.call-done = bf16[1024,4096]{1,0:T(8,128)(2,1)} async-done(((bf16[16,4096]{1,0:T(8,128)(2,1)}), bf16[1024,4096]{1,0:T(8,128)(2,1)}) %all-gather.4.cloned.1.call-update) | async-done | bytes 8388624 | tf_op jit(solution)/shard_map/all_gather | solution.py:34
  214.9 7.6 %fusion.6 = f32[1024,224]{0,1:T(8,128)} fusion(bf16[1024,4096]{1,0:T(8,128)(2,1)} %all-gather.4.cloned.1.call-done, bf16[1,224,4096]{2,1,0:T(8,128)(2,1)} %param.13), kind=kOutput, calls=%fused_computation.12 | convolution fusion | flops 1879048192 | bytes 11141120 | tf_op jit(solution)/shard_map/dot_general | solution.py:17
  222.5 3.6 fusion.47
  226.1 16.0 %all-gather.8.cloned.1.call-done = bf16[224,4096]{1,0:T(8,128)(2,1)} async-done(((bf16[224,1024]{1,0:T(8,128)(2,1)}), bf16[224,4096]{1,0:T(8,128)(2,1)}) %all-gather.8.cloned.1.call-update) | async-done | bytes 1835024 | tf_op jit(solution)/shard_map/all_gather | solution.py:30
  242.1 7.1 %fusion.10 = f32[1024]{0:T(1024)S(1)} fusion(bf16[1024,224]{0,1:T(8,128)(2,1)S(1)} %copy-done.8, bf16[1024,4096]{1,0:T(8,128)(2,1)} %all-gather.4.cloned.1.call-done, bf16[224,4096]{1,0:T(8,128)(2,1)} %all-gather.8.cloned.1.call-done, f32[1024,224]{0,1:T(8,128)} %fusion.47), kind=kOutput, calls=%fused_computation.20 | convolution fusion | flops 1881340928 | bytes 11603968 | tf_op jit(solution)/shard_map/dot_general | solution.py:17
  249.2 7.1 %fusion.19 = (f32[1024]{0:T(1024)S(1)}, f32[1024,224]{0,1:T(8,128)}) fusion(bf16[1024,224]{0,1:T(8,128)(2,1)S(1)} %copy-done.8, f32[1024,224]{0,1:T(8,128)S(1)} %copy-done.10, bf16[1024,4096]{1,0:T(8,128)(2,1)} %all-gather.4.cloned.1.call-done, bf16[1,224,4096]{2,1,0:T(8,128)(2,1)S(1)} %copy-done), kind=kOutput, calls=%fused_computation.32 | convolution fusion | flops 1881340928 | bytes 12521472 | tf_op jit(solution)/shard_map/dot_general | solution.py:17
  256.7 184.5 %all-reduce = (f32[64]{0:T(128)S(1)}, f32[64]{0:T(128)S(1)}) all-reduce(f32[64]{0:T(128)S(1)} %reduce_sum.46, f32[64]{0:T(128)S(1)} %reduce_sum.48), channel_id=1, replica_groups=mesh['rep'=4,'fsdp'=64] {'fsdp'}, use_global_device_ids=true, to_apply=%region_2.3 | all-reduce | flops 128 | bytes 1024 | tf_op jit(solution)/shard_map/psum | solution.py:44
  441.4 0.8 fusion.35
  443.3 7.2 %fusion.1 = bf16[1,224,4096]{2,1,0:T(8,128)(2,1)} fusion(bf16[1024,4096]{1,0:T(8,128)(2,1)} %all-gather.4.cloned.1.call-done, bf16[1024,224]{0,1:T(8,128)(2,1)S(1)} %copy-done.8, f32[1024]{0:T(1024)S(1)} %convert_multiply_fusion.4, f32[1024,224]{0,1:T(8,128)} %fusion.6), kind=kOutput, calls=%fused_computation.3 | convolution fusion | flops 1881800704 | bytes 11603968 | tf_op jit(solution)/shard_map/dot_general | solution.py:72
  450.5 6.9 %fusion = bf16[1,224,4096]{2,1,0:T(8,128)(2,1)} fusion(bf16[1024,4096]{1,0:T(8,128)(2,1)} %all-gather.4.cloned.1.call-done, f32[1024,224]{0,1:T(8,128)S(1)} %copy-done.12, bf16[1024,224]{0,1:T(8,128)(2,1)S(1)} %copy-done.8, f32[1024,224]{0,1:T(8,128)S(1)} %copy-done.11, f32[1024]{0:T(1024)S(1)} %convert_multiply_fusion.4), kind=kOutput, calls=%fused_computation.2 | convolution fusion | flops 1882718208 | bytes 12521472 | tf_op jit(solution)/shard_map/dot_general | solution.py:69
  (41 shorter events, 1.4 us)
Async XLA Ops:
  8.0 241.2 %copy-start = (bf16[1,224,4096]{2,1,0:T(8,128)(2,1)S(1)}, bf16[1,224,4096]{2,1,0:T(8,128)(2,1)}, u32[]{:S(2)}) copy-start(bf16[1,224,4096]{2,1,0:T(8,128)(2,1)} %param.14) | copy-start | bytes 5505028
  8.0 33.4 %all-gather.6.cloned.1.call-start = ((), (), s32[]{:S(2)}) async-start(), calls=%async_computation.2 | async-start | bytes 2293760 | tf_op jit(solution)/shard_map/all_gather | solution.py:29
  8.7 78.3 %reduce-scatter.2.cloned.1.call-start = ((), (), s32[]{:S(2)}) async-start(), calls=%async_computation.4 | async-start | bytes 2293760 | tf_op jit(solution)/shard_map/reduce_scatter | solution.py:82
  49.7 1.5 copy-start.1
  49.7 2.0 copy-start.2
  51.7 5.5 %copy-start.9 = (s32[1,64]{1,0:T(1,128)S(1)}, s32[1,64]{1,0:T(1,128)}, u32[]{:S(2)}) copy-start(s32[1,64]{1,0:T(1,128)} %param.12) | copy-start | bytes 772
  51.7 35.3 %copy-start.4 = (bf16[224,1024]{1,0:T(8,128)(2,1)S(1)}, bf16[224,1024]{1,0:T(8,128)(2,1)}, u32[]{:S(2)}) copy-start(bf16[224,1024]{1,0:T(8,128)(2,1)} %param.15) | copy-start | bytes 1376260
  51.7 35.3 %copy-start.5 = (f32[224,1024]{1,0:T(8,128)S(1)}, f32[224,1024]{1,0:T(8,128)}, u32[]{:S(2)}) copy-start(f32[224,1024]{1,0:T(8,128)} %param.17) | copy-start | bytes 2752516
  56.1 158.8 %all-gather.4.cloned.1.call-start = ((), (), s32[]{:S(2)}) async-start(), calls=%async_computation.1 | async-start | bytes 8519680 | tf_op jit(solution)/shard_map/all_gather | solution.py:34
  56.7 185.4 %all-gather.8.cloned.1.call-start = ((), (), s32[]{:S(2)}) async-start(), calls=%async_computation.3 | async-start | bytes 2293760 | tf_op jit(solution)/shard_map/all_gather | solution.py:30
  214.9 7.6 %copy-start.3 = (bf16[224,4096]{1,0:T(8,128)(2,1)S(1)}, bf16[224,4096]{1,0:T(8,128)(2,1)}, u32[]{:S(2)}) copy-start(bf16[224,4096]{1,0:T(8,128)(2,1)} %all-gather.6.cloned.1.call-done) | copy-start | bytes 5505028
  214.9 7.6 %copy-start.7 = (bf16[1024,4096]{1,0:T(8,128)(2,1)S(1)}, bf16[1024,4096]{1,0:T(8,128)(2,1)}, u32[]{:S(2)}) copy-start(bf16[1024,4096]{1,0:T(8,128)(2,1)} %all-gather.4.cloned.1.call-done) | copy-start | bytes 25165828
  222.5 19.6 %copy-start.8 = (bf16[1024,224]{0,1:T(8,128)(2,1)S(1)}, bf16[1024,224]{0,1:T(8,128)(2,1)}, u32[]{:S(2)}) copy-start(bf16[1024,224]{0,1:T(8,128)(2,1)} %param.10) | copy-start | bytes 1376260
  242.1 7.1 %copy-start.10 = (f32[1024,224]{0,1:T(8,128)S(1)}, f32[1024,224]{0,1:T(8,128)}, u32[]{:S(2)}) copy-start(f32[1024,224]{0,1:T(8,128)} %fusion.6) | copy-start | bytes 2752516
  249.2 7.2 %copy-start.6 = (s32[1024]{0:T(1024)S(1)}, s32[1024]{0:T(1024)}, u32[]{:S(2)}) copy-start(s32[1024]{0:T(1024)} %param.11) | copy-start | bytes 12292
  443.3 7.2 %copy-start.11 = (f32[1024,224]{0,1:T(8,128)S(1)}, f32[1024,224]{0,1:T(8,128)}, u32[]{:S(2)}) copy-start(f32[1024,224]{0,1:T(8,128)} %fusion.6) | copy-start | bytes 2752516
  443.3 7.2 %copy-start.12 = (f32[1024,224]{0,1:T(8,128)S(1)}, f32[1024,224]{0,1:T(8,128)}, u32[]{:S(2)}) copy-start(f32[1024,224]{0,1:T(8,128)} %get-tuple-element.12) | copy-start | bytes 2752516
Sparse Core Ops, SparseCore 0:
  10.7 30.7 all-gather.5
  56.2 30.7 reduce-scatter.1
Sparse Core Ops, SparseCore 1:
  60.1 154.7 all-gather.3
  216.5 25.5 all-gather.7
where the time goes:
time: 466 us
  waiting for transfers between devices  205 us (44%)
  blocking collectives  185 us (40%)
  matrix products  40.7 us (9%)
  between operations  17.4 us (4%)
  other arithmetic  12.8 us (3%)
  local copies, waits for them, and re-layouts  5.06 us (1%)
    psum x1, blocking collectives, per_device(): lax.psum((local_scores(hidden, readout, mask_f, seqs), local_scores(hidde...  185 us
    all_gather x1, waiting for transfers between devices, per_device(): inputs = lax.all_gather(tokens, 'fsdp', axis=0, tiled=True)  125 us
    all_gather x1, waiting for transfers between devices, per_device(): lax.all_gather(outer_gate, 'rep', axis=1, tiled=True)  32.6 us
    reduce_scatter x1, waiting for transfers between devices, per_device(): lax.psum_scatter(terms.astype(jnp.bfloat16), 'rep', scatter_dimension=1,...  29.5 us
    dot_general x4, matrix products, project(): lax.dot_general(rows, weight, (((1,), (1,)), ((), ())), preferred_element...  25.4 us
    all_gather x1, waiting for transfers between devices, per_device(): lax.all_gather(outer_up, 'rep', axis=1, tiled=True)  16 us
  transfers between devices with their start and end apart: 4, of which 4 were waited for; matrix products, arithmetic and copies ran while one was open for 3% of the time, Pallas kernels for 0%

commit v1 on v0

v1 whole, which is shorter than its diff:
```python
import functools
import heapq

import jax
import jax.numpy as jnp
import numpy as np
from jax import lax
from jax.experimental import pallas as pl
from jax.experimental.pallas import tpu as pltpu
from jax.sharding import PartitionSpec as P

BLOCK = 128
LEN = 16
NZ, NX, NY = 8, 2, 4
SEQS = NZ * NX * NY
GROUP_TOK = SEQS * LEN
CHUNK = 256
CHUNKS = GROUP_TOK // CHUNK
PER_CHUNK = CHUNK // LEN

dpo_beta = 0.1
outer_rate = 0.7
outer_mu = 0.9
tiny_eps = 1e-06

MESH = pl.DeviceIdType.MESH
F32 = jnp.float32
BF16 = jnp.bfloat16


def gather_plan():
    arrives = {}
    flip = 0
    for dx in range(NX):
        for dz in range(NZ):
            for dy in range(NY):
                if (dx, dy, dz) == (0, 0, 0):
                    continue
                if dy == 0 and dz == 0:
                    side = "x"
                elif dz != 0 and (dy == 0 or (dx == 0 and dz != 4)):
                    side = "z+" if dz < 4 or (dz == 4 and dx == 0) else "z-"
                elif dy == 2:
                    side = "y+" if flip % 2 == 0 else "y-"
                    flip += 1
                else:
                    side = "y+" if dy == 1 else "y-"
                arrives[(dx, dy, dz)] = side
    return arrives


ARRIVES = gather_plan()


def source(s):
    dx, dy, dz = s
    side = ARRIVES[s]
    if side == "x":
        return (dx ^ 1, dy, dz)
    if side[0] == "y":
        return (dx, (dy + (-1 if side == "y+" else 1)) % NY, dz)
    return (dx, dy, (dz + (-1 if side == "z+" else 1)) % NZ)


def gather_order(wire=2.82, hop=1.7, far=2.5):
    children = {}
    for s in ARRIVES:
        children.setdefault(source(s), []).append(s)

    def depth(s):
        return 1 + max([depth(k) for k in children.get(s, [])], default=0)

    def size(s):
        return 1 + sum(size(k) for k in children.get(s, []))

    sides = ("x", "y+", "y-", "z+", "z-")
    waiting = {side: [] for side in sides}
    busy = {side: False for side in sides}
    events = [(0.0, 0, "arrive", (0, 0, 0))]
    count = 1
    order = []
    while events:
        now, _, kind, what = heapq.heappop(events)
        if kind == "free":
            busy[what] = False
        else:
            order.append(what)
            for k in children.get(what, []):
                waiting[ARRIVES[k]].append(k)
        for side in sides:
            if not busy[side] and waiting[side]:
                waiting[side].sort(key=lambda s: (-depth(s), -size(s)))
                s = waiting[side].pop(0)
                busy[side] = True
                heapq.heappush(events, (now + wire, count, "free", side))
                heapq.heappush(
                    events, (now + wire + (far if side == "x" else hop), count + 1, "arrive", s)
                )
                count += 2
    for kids in children.values():
        kids.sort(key=lambda s: (-depth(s), -size(s)))
    return order, children


ORDER, CHILDREN = gather_order()
RANK = {s: i for i, s in enumerate(ORDER)}


def position_codes():
    codes = np.zeros((1, GROUP_TOK), np.int32)
    for (dx, dy, dz), rank in RANK.items():
        codes[0, rank * LEN:(rank + 1) * LEN] = dz * 8 + dx * 4 + dy
    return codes


def sequence_of(codes):
    me = lax.axis_index("fsdp")
    z, x, y = me // 8, (me // 4) % 2, me % 4
    dz, dx, dy = codes >> 3, (codes >> 2) & 1, codes & 3
    return (((dz + z) & 7) << 3) + (((dx + x) & 1) << 2) + ((dy + y) & 3)


def iota(shape, axis):
    return lax.broadcasted_iota(jnp.int32, shape, axis)


def column_to_row(column, rows, lanes):
    eye = iota((rows, lanes), 0) == iota((rows, lanes), 1)
    return jnp.sum(jnp.where(eye, column, 0.0), axis=0, keepdims=True)


def row_to_column(row, rows, lanes):
    eye = iota((rows, lanes), 0) == iota((rows, lanes), 1)
    return jnp.sum(jnp.where(eye, row, 0.0), axis=1, keepdims=True)


def gather_kernel(
    codes_ref, mask_ref, tokens_hbm, readout_hbm, wg_hbm, wu_hbm, og_hbm, ou_hbm,
    x_out, grads_out, average_out, relative_out,
    x_all, wg, wu, og, ou, own, slabs, readout, grads, average, gate_s, upper_s, token_score,
    near, wide, near_own, wide_own,
    local_sem, send_sem, recv_sem, rep_send, rep_recv, sum_send, sum_recv, out_sem,
):
    units = wg.shape[0]
    width = og.shape[1]
    part = own.shape[1]
    rep = lax.axis_index("rep")
    me = lax.axis_index("fsdp")
    z, x, y = me // 8, (me // 4) % 2, me % 4

    def at(dx, dy, dz):
        return ((z + dz) % 8) * 8 + ((x + dx) % 2) * 4 + (y + dy) % 4

    barrier = pltpu.get_barrier_semaphore()
    peers = [(rep, at(0, 0, d)) for d in range(1, NZ)]
    peers += [(rep, at(d // 4, d % 4, 0)) for d in range(1, NX * NY)]
    peers += [(rep ^ d, me) for d in range(1, 4)]
    for peer in peers:
        pl.semaphore_signal(barrier, inc=1, device_id=peer, device_id_type=MESH)

    def columns(r):
        return pl.ds(pl.multiple_of(r * part, part), part)

    local = [
        pltpu.make_async_copy(tokens_hbm, x_all.at[pl.ds(0, LEN), :], local_sem.at[0]),
        pltpu.make_async_copy(readout_hbm, readout, local_sem.at[1]),
        pltpu.make_async_copy(wg_hbm, wg, local_sem.at[2]),
        pltpu.make_async_copy(wu_hbm, wu, local_sem.at[3]),
        pltpu.make_async_copy(og_hbm, own, local_sem.at[4]),
        pltpu.make_async_copy(og_hbm, og.at[:, columns(rep)], local_sem.at[5]),
        pltpu.make_async_copy(ou_hbm, ou.at[:, columns(rep)], local_sem.at[6]),
        pltpu.make_async_copy(wg_hbm.at[:, columns(rep)], slabs.at[0], local_sem.at[7]),
    ]
    for copy in local:
        copy.start()
    pl.semaphore_wait(barrier, len(peers))

    back = {"x": (1, 0, 0), "y+": (0, -1, 0), "y-": (0, 1, 0), "z+": (0, 0, -1), "z-": (0, 0, 1)}

    def shard_copy(s):
        origin = source(s)
        rank = RANK[s]
        src = tokens_hbm if origin == (0, 0, 0) else x_all.at[pl.ds(RANK[origin] * LEN, LEN), :]
        return pltpu.make_async_remote_copy(
            src_ref=src,
            dst_ref=x_all.at[pl.ds(rank * LEN, LEN), :],
            send_sem=send_sem.at[rank],
            recv_sem=recv_sem.at[rank],
            device_id=(rep, at(*back[ARRIVES[s]])),
            device_id_type=MESH,
        )

    copies = {s: shard_copy(s) for s in ARRIVES}

    def rep_copy(i, src, dst, distance):
        return pltpu.make_async_remote_copy(
            src_ref=src, dst_ref=dst, send_sem=rep_send.at[i], recv_sem=rep_recv.at[i],
            device_id=(rep ^ distance, me), device_id_type=MESH,
        )

    mine, across = columns(rep), columns(rep ^ 2)
    gate_far = rep_copy(0, og_hbm, og.at[:, mine], 2)
    up_far = rep_copy(1, ou_hbm, ou.at[:, mine], 2)
    gate_near = rep_copy(2, og_hbm, og.at[:, mine], 1)
    up_near = rep_copy(3, ou_hbm, ou.at[:, mine], 1)
    gate_pass = rep_copy(4, og.at[:, across], og.at[:, across], 1)
    up_pass = rep_copy(5, ou.at[:, across], ou.at[:, across], 1)
    slab_copies = [
        rep_copy(5 + d, wg_hbm.at[:, columns(rep ^ d)], slabs.at[d], d) for d in (1, 2, 3)
    ]

    for s in CHILDREN[(0, 0, 0)]:
        copies[s].start()
    for copy in (gate_far, gate_near, up_far, up_near, slab_copies[0], slab_copies[1], slab_copies[2]):
        copy.start()

    local[1].wait()
    masked = (readout[...].astype(F32) * mask_ref[...].astype(F32)).astype(BF16)
    sequence = sequence_of(codes_ref[...])
    wanted = sequence * LEN + (iota((1, GROUP_TOK), 1) & (LEN - 1))
    for c in range(CHUNKS):
        lanes = slice(c * CHUNK, (c + 1) * CHUNK)
        pick = (iota((GROUP_TOK, CHUNK), 0) == wanted[:, lanes]).astype(F32).astype(BF16)
        readout[:, lanes] = jnp.dot(masked, pick, preferred_element_type=F32).astype(BF16)
    token_score[...] = jnp.zeros_like(token_score)
    for i in (2, 3):
        local[i].wait()

    def project(weight, c):
        return lax.dot_general(
            weight[...], x_all[pl.ds(c * CHUNK, CHUNK), :], (((1,), (1,)), ((), ())),
            preferred_element_type=F32,
        )

    ROWS = 32

    def unit_gate(weight, c):
        gate_s[...] = project(weight, c)

    def unit_upper(weight, c):
        upper_s[...] = project(weight, c)

    def unit_policy(c):
        lanes = pl.ds(c * CHUNK, CHUNK)

        def body(i, total):
            rows = pl.ds(pl.multiple_of(i * ROWS, ROWS), ROWS)
            gate, upper = gate_s[rows, :], upper_s[rows, :]
            read = readout[rows, lanes].astype(F32)
            sigma = jax.nn.sigmoid(gate)
            silu = gate * sigma
            hidden = (silu * upper).astype(BF16).astype(F32)
            grads[rows, lanes] = read * upper * sigma * (1.0 + gate * (1.0 - sigma))
            grads[pl.ds(pl.multiple_of(units + i * ROWS, ROWS), ROWS), lanes] = read * silu
            return total + jnp.sum(hidden * read, axis=0, keepdims=True)

        total = lax.fori_loop(0, units // ROWS, body, jnp.zeros((1, CHUNK), F32))
        token_score[:, lanes] += total

    def unit_reference(c):
        lanes = pl.ds(c * CHUNK, CHUNK)

        def body(i, total):
            rows = pl.ds(pl.multiple_of(i * ROWS, ROWS), ROWS)
            gate, upper = gate_s[rows, :], upper_s[rows, :]
            read = readout[rows, lanes].astype(F32)
            hidden = (gate * jax.nn.sigmoid(gate) * upper).astype(BF16).astype(F32)
            return total + jnp.sum(hidden * read, axis=0, keepdims=True)

        total = lax.fori_loop(0, units // ROWS, body, jnp.zeros((1, CHUNK), F32))
        token_score[:, lanes] -= total

    def policy_units(c):
        return [
            functools.partial(unit_gate, wg, c),
            functools.partial(unit_upper, wu, c),
            functools.partial(unit_policy, c),
        ]

    def reference_units(c):
        return [
            functools.partial(unit_gate, og, c),
            functools.partial(unit_upper, ou, c),
            functools.partial(unit_reference, c),
        ]

    outs = [
        pltpu.make_async_copy(
            x_all.at[pl.ds(c * CHUNK, CHUNK), :], x_out.at[pl.ds(c * CHUNK, CHUNK), :], out_sem.at[c]
        )
        for c in range(CHUNKS)
    ]

    todo = []
    local[0].wait()
    for rank in range(1, SEQS):
        s = ORDER[rank]
        copies[s].wait_recv()
        for child in CHILDREN.get(s, []):
            copies[child].start()
        if rank == 20:
            gate_far.wait_recv()
            gate_pass.start()
        if rank == 36:
            up_far.wait_recv()
            up_pass.start()
        if rank == 40:
            local[5].wait()
            local[6].wait()
            for copy in (gate_near, up_near, gate_pass, up_pass):
                copy.wait_recv()
            todo += reference_units(0) + reference_units(1)
        if rank % PER_CHUNK == PER_CHUNK - 1:
            c = rank // PER_CHUNK
            outs[c].start()
            todo += policy_units(c)
            if c >= 2:
                todo += reference_units(c)
        if todo:
            todo.pop(0)()
    for unit in todo:
        unit()

    grads_copy = pltpu.make_async_copy(grads, grads_out, out_sem.at[CHUNKS])
    grads_copy.start()

    belongs = iota((SEQS, GROUP_TOK), 0) == sequence
    partial = jnp.sum(jnp.where(belongs, token_score[...], 0.0), axis=1, keepdims=True)
    partial = column_to_row(partial, SEQS, BLOCK)
    near_own[...] = partial
    near_copies = [
        pltpu.make_async_remote_copy(
            src_ref=near_own, dst_ref=near.at[z], send_sem=sum_send.at[d], recv_sem=sum_recv.at[z],
            device_id=(rep, at(0, 0, d)), device_id_type=MESH,
        )
        for d in (4, 3, 5, 2, 6, 1, 7)
    ]
    for copy in near_copies:
        copy.start()
    near[z] = partial

    for copy in slab_copies:
        copy.wait_recv()
    local[4].wait()
    local[7].wait()
    STEP = 16

    def pseudo(i, _):
        rows = pl.ds(pl.multiple_of(i * STEP, STEP), STEP)
        for b in range(part // BLOCK):
            lanes = slice(b * BLOCK, (b + 1) * BLOCK)
            outer = own[rows, lanes].astype(F32)
            total = jnp.zeros((STEP, BLOCK), F32)
            for r in range(4):
                delta = outer - slabs[r, rows, lanes].astype(F32)
                scale = jnp.max(jnp.abs(delta), axis=1, keepdims=True) + tiny_eps
                scale = scale.astype(BF16).astype(F32)
                total += (delta / scale).astype(BF16).astype(F32) * scale
            average[rows, lanes] = total * 0.25
        return 0

    half = units // STEP // 2
    lax.fori_loop(0, half, pseudo, 0)

    for d in range(1, NZ):
        pltpu.make_async_remote_copy(
            src_ref=near_own, dst_ref=near.at[(z + d) % 8], send_sem=sum_send.at[d],
            recv_sem=sum_recv.at[(z + d) % 8], device_id=(rep, at(0, 0, d)), device_id_type=MESH,
        ).wait_recv()
    partial = near[0]
    for i in range(1, NZ):
        partial = partial + near[i]
    plane = x * 4 + y
    wide_own[...] = partial
    wide_copies = [
        pltpu.make_async_remote_copy(
            src_ref=wide_own, dst_ref=wide.at[plane], send_sem=sum_send.at[8 + d],
            recv_sem=sum_recv.at[8 + plane], device_id=(rep, at(d // 4, d % 4, 0)), device_id_type=MESH,
        )
        for d in (6, 5, 7, 2, 4, 1, 3)
    ]
    for copy in wide_copies:
        copy.start()
    wide[plane] = partial

    lax.fori_loop(half, units // STEP, pseudo, 0)
    average_copy = pltpu.make_async_copy(average, average_out, out_sem.at[CHUNKS + 1])
    average_copy.start()

    for d in range(1, NX * NY):
        other = ((x + d // 4) % 2) * 4 + (y + d % 4) % 4
        pltpu.make_async_remote_copy(
            src_ref=wide_own, dst_ref=wide.at[other], send_sem=sum_send.at[8 + d],
            recv_sem=sum_recv.at[8 + other], device_id=(rep, at(d // 4, d % 4, 0)), device_id_type=MESH,
        ).wait_recv()
    partial = wide[0]
    for i in range(1, NX * NY):
        partial = partial + wide[i]
    relative_out[...] = partial

    for s in ORDER[1:]:
        copies[s].wait_send()
    for copy in (gate_far, up_far, gate_near, up_near, gate_pass, up_pass, *slab_copies):
        copy.wait_send()
    for copy in near_copies + wide_copies:
        copy.wait_send()
    for copy in outs:
        copy.wait()
    grads_copy.wait()
    average_copy.wait()


def gather_forward(codes, mask, tokens, readout_t, w_gate, w_up, outer_gate, outer_up):
    units, width = w_gate.shape
    part = outer_gate.shape[1]
    any_spec = pl.BlockSpec(memory_space=pl.ANY)
    vmem_spec = pl.BlockSpec(memory_space=pltpu.VMEM)
    return pl.pallas_call(
        gather_kernel,
        name="gather_forward",
        out_shape=(
            jax.ShapeDtypeStruct((GROUP_TOK, width), BF16),
            jax.ShapeDtypeStruct((2 * units, GROUP_TOK), F32),
            jax.ShapeDtypeStruct((units, part), F32),
            jax.ShapeDtypeStruct((1, BLOCK), F32),
        ),
        in_specs=[vmem_spec] * 2 + [any_spec] * 6,
        out_specs=(any_spec, any_spec, any_spec, vmem_spec),
        scratch_shapes=[
            pltpu.VMEM((GROUP_TOK, width), BF16),
            pltpu.VMEM((units, width), BF16),
            pltpu.VMEM((units, width), BF16),
            pltpu.VMEM((units, width), BF16),
            pltpu.VMEM((units, width), BF16),
            pltpu.VMEM((units, part), BF16),
            pltpu.VMEM((4, units, part), BF16),
            pltpu.VMEM((units, GROUP_TOK), BF16),
            pltpu.VMEM((2 * units, GROUP_TOK), F32),
            pltpu.VMEM((units, part), F32),
            pltpu.VMEM((units, CHUNK), F32),
            pltpu.VMEM((units, CHUNK), F32),
            pltpu.VMEM((1, GROUP_TOK), F32),
            pltpu.VMEM((NZ, 1, BLOCK), F32),
            pltpu.VMEM((NX * NY, 1, BLOCK), F32),
            pltpu.VMEM((1, BLOCK), F32),
            pltpu.VMEM((1, BLOCK), F32),
            pltpu.SemaphoreType.DMA((8,)),
            pltpu.SemaphoreType.DMA((SEQS,)),
            pltpu.SemaphoreType.DMA((SEQS,)),
            pltpu.SemaphoreType.DMA((9,)),
            pltpu.SemaphoreType.DMA((9,)),
            pltpu.SemaphoreType.DMA((16,)),
            pltpu.SemaphoreType.DMA((16,)),
            pltpu.SemaphoreType.DMA((CHUNKS + 2,)),
        ],
        compiler_params=pltpu.CompilerParams(collective_id=0, has_side_effects=True),
    )(codes, mask, tokens, readout_t, w_gate, w_up, outer_gate, outer_up)


def backward_kernel(
    codes_ref, order_ref, relative_ref, grads_ref, x_ref, average_ref, outer_ref, moment_ref,
    loss_out, gate_out, up_out, outer_out, moment_out,
    rows_s,
):
    units = gate_out.shape[1]
    pairs = SEQS // 2

    @pl.when(pl.program_id(0) == 0)
    def _():
        relative = row_to_column(relative_ref[...], SEQS, BLOCK)
        placed = iota((SEQS, SEQS), 0) == order_ref[...]
        by_place = jnp.sum(jnp.where(placed, relative, 0.0), axis=0, keepdims=True)
        place, pair = iota((pairs, SEQS), 1), iota((pairs, SEQS), 0)
        chosen, rejected = place == 2 * pair, place == 2 * pair + 1
        sign = jnp.where(chosen, 1.0, jnp.where(rejected, -1.0, 0.0))
        margin = dpo_beta * jnp.sum(sign * by_place, axis=1, keepdims=True)
        loss_out[0] = jnp.sum(jax.nn.softplus(-margin)) / pairs
        weight = dpo_beta * jax.nn.sigmoid(-margin) / pairs
        place_coef = jnp.sum(-sign * weight, axis=0, keepdims=True)
        coef = jnp.sum(jnp.where(placed, place_coef, 0.0), axis=1, keepdims=True)
        belongs = iota((SEQS, GROUP_TOK), 0) == sequence_of(codes_ref[...])
        token_grad = jnp.sum(jnp.where(belongs, coef, 0.0), axis=0, keepdims=True)
        rows_s[...] = (grads_ref[...] * token_grad).astype(BF16)

    out = jnp.dot(rows_s[...], x_ref[...], preferred_element_type=F32).astype(BF16)
    gate_out[0] = out[:units]
    up_out[0] = out[units:]
    average = average_ref[...]
    new_moment = outer_mu * moment_ref[...] + average
    moment_out[...] = new_moment
    outer_out[...] = (
        outer_ref[...].astype(F32) - outer_rate * (average + outer_mu * new_moment)
    ).astype(BF16)


def backward(codes, order, relative, grads, x_all, average, outer_gate, moment):
    units, part = outer_gate.shape
    width = x_all.shape[1]
    steps = 8
    block, slab = width // steps, part // steps
    whole = lambda i: (0, 0)
    column = lambda i: (0, i)
    once = pl.Buffered(1)
    return pl.pallas_call(
        backward_kernel,
        name="backward",
        grid=(steps,),
        out_shape=(
            jax.ShapeDtypeStruct((1,), F32),
            jax.ShapeDtypeStruct((1, units, width), BF16),
            jax.ShapeDtypeStruct((1, units, width), BF16),
            jax.ShapeDtypeStruct((units, part), BF16),
            jax.ShapeDtypeStruct((units, part), F32),
        ),
        in_specs=[
            pl.BlockSpec(codes.shape, whole),
            pl.BlockSpec(order.shape, whole),
            pl.BlockSpec(relative.shape, whole),
            pl.BlockSpec(grads.shape, whole, pipeline_mode=once),
            pl.BlockSpec((GROUP_TOK, block), column),
            pl.BlockSpec((units, slab), column),
            pl.BlockSpec((units, slab), column),
            pl.BlockSpec((units, slab), column),
        ],
        out_specs=(
            pl.BlockSpec(memory_space=pltpu.SMEM),
            pl.BlockSpec((1, units, block), lambda i: (0, 0, i)),
            pl.BlockSpec((1, units, block), lambda i: (0, 0, i)),
            pl.BlockSpec((units, slab), column),
            pl.BlockSpec((units, slab), column),
        ),
        scratch_shapes=[pltpu.VMEM((2 * units, GROUP_TOK), BF16)],
        compiler_params=pltpu.CompilerParams(dimension_semantics=("arbitrary",)),
    )(codes, order, relative, grads, x_all, average, outer_gate, moment)


def per_device(tokens, readout, resp_mask, order, w_gate, w_up, outer_gate, outer_up, moment):
    codes = jnp.asarray(position_codes())
    x_all, grads, average, relative = gather_forward(
        codes, resp_mask.reshape(1, -1), tokens, readout.T, w_gate[0], w_up[0], outer_gate, outer_up
    )
    return backward(codes, order, relative, grads, x_all, average, outer_gate, moment)


def solution(mesh):
    return jax.shard_map(
        per_device,
        mesh=mesh,
        in_specs=(
            P(("rep", "fsdp"), None),
            P("rep", "fsdp"),
            P("rep"),
            P("rep", None),
            P("rep", "fsdp", None),
            P("rep", "fsdp", None),
            P("fsdp", "rep"),
            P("fsdp", "rep"),
            P("fsdp", "rep"),
        ),
        out_specs=(
            P("rep"),
            P("rep", "fsdp", None),
            P("rep", "fsdp", None),
            P("fsdp", "rep"),
            P("fsdp", "rep"),
        ),
        check_vma=False,
    )
```

time: 466 us -> 98.4 us (0.21)
  waiting for transfers between devices: 205 us -> 0 us
  blocking collectives: 185 us -> 0 us
  Pallas kernels: 0 us -> 97.4 us
  matrix products: 40.7 us -> 0 us
  between operations: 17.4 us -> 0.64 us
  other arithmetic: 12.8 us -> 0 us
  local copies, waits for them, and re-layouts: 5.06 us -> 0 us
    psum x1 -> x0, blocking collectives: 185 us -> none  [per_device(): lax.psum((local_scores(hidden, readout, mask_f, seqs), local_scores(hidde...]
    all_gather x3 -> x0, waiting for transfers between devices: 174 us -> none  [the longest x1 125 us: per_device(): inputs = lax.all_gather(tokens, 'fsdp', axis=0, tiled=True)]
    pallas_call x0 -> x2, Pallas kernels: none -> 97.4 us  [the longest x1 86.2 us: gather_forward(): pl.pallas_call(gather_kernel, name='gather_forward', out_shape=(jax.Shape...]
    dot_general x9 -> x0, matrix products: 40.7 us -> none  [the longest x4 25.4 us: project(): lax.dot_general(rows, weight, (((1,), (1,)), ((), ())), preferred_element...]
    reduce_scatter x1 -> x0, waiting for transfers between devices: 29.5 us -> none  [per_device(): lax.psum_scatter(terms.astype(jnp.bfloat16), 'rep', scatter_dimension=1,...]
    convert_element_type x3 -> x0, other arithmetic: 6.73 us -> none  [the longest x1 4.34 us: per_device(): terms.astype(jnp.bfloat16)]
  transfers between devices with their start and end apart: 4 -> 0, of which waited for: 4 -> 0; matrix products, arithmetic and copies ran while one was open for 3% -> 0% of each run, Pallas kernels for 0% -> 0%
where the time goes in v1:
time: 98.4 us; the launch traced here: 98.1 us
  Pallas kernels  97.4 us (99%)
    pallas_call x1, Pallas kernels, gather_forward(): pl.pallas_call(gather_kernel, name='gather_forward', out_shape=(jax.Shape...  86.2 us
    pallas_call x1, Pallas kernels, backward(): pl.pallas_call(backward_kernel, name='backward', grid=(steps,), out_shape...  11.3 us

profile of v1, /device:TPU:2, one launch (start us, length us, event | category | flops | bytes accessed | tf_op | source)
XLA Modules:
  0.0 98.1 jit_solution(6220803758979864319)
XLA Ops:
  0.6 86.2 %gather_forward.1 = (bf16[1024,4096]{1,0:T(8,128)(2,1)}, f32[448,1024]{1,0:T(8,128)}, f32[224,1024]{1,0:T(8,128)}, f32[1,128]{1,0:T(1,128)}) custom-call(s32[1,1024]{1,0:T(1,128)} %constant.2.clone.codes_ref, s32[1,1024]{1,0:T(1,128)} %bitcast.7, bf16[16,4096]{1,0:T(8,128)(2,1)} %tokens_hbm.1, bf16[224,1024]{1,0:T(8,128)(2,1)} %bitcast.6, ...), custom_call_target="tpu_custom_call" | custom-call | tf_op jit(solution)/shard_map/gather_forward/pallas_call | solution.py:418
  86.8 11.3 %backward.1 = (f32[1]{0:T(128)}, bf16[1,224,4096]{2,1,0:T(8,128)(2,1)}, bf16[1,224,4096]{2,1,0:T(8,128)(2,1)}, bf16[224,1024]{1,0:T(8,128)(2,1)}, f32[224,1024]{1,0:T(8,128)}) custom-call(s32[1,1024]{1,0:T(1,128)} %constant.2.clone.codes_ref, s32[1,64]{1,0:T(1,128)} %order_ref.1, f32[1,128]{1,0:T(1,128)} %get-tuple-element.9.relative_ref, ...), custom_call_target="tpu_custom_call" | custom-call | tf_op jit(solution)/shard_map/backward/pallas_call | solution.py:504

commit v2 on v1

--- a/solution.py
+++ b/solution.py
@@ -17,6 +17,7 @@
 CHUNK = 256
 CHUNKS = GROUP_TOK // CHUNK
 PER_CHUNK = CHUNK // LEN
+PIECES = 2
 
 dpo_beta = 0.1
 outer_rate = 0.7
@@ -38,7 +39,7 @@
                     continue
                 if dy == 0 and dz == 0:
                     side = "x"
-                elif dz != 0 and (dy == 0 or (dx == 0 and dz != 4)):
+                elif dz != 0 and (dy == 0 or (dx == 1 and dz != 4)):
                     side = "z+" if dz < 4 or (dz == 4 and dx == 0) else "z-"
                 elif dy == 2:
                     side = "y+" if flip % 2 == 0 else "y-"
@@ -62,7 +63,7 @@
     return (dx, dy, (dz + (-1 if side == "z+" else 1)) % NZ)
 
 
-def gather_order(wire=2.82, hop=1.7, far=2.5):
+def gather_order(wire=2.73 / PIECES, hop=2.2, far=3.0):
     children = {}
     for s in ARRIVES:
         children.setdefault(source(s), []).append(s)
@@ -70,40 +71,28 @@
     def depth(s):
         return 1 + max([depth(k) for k in children.get(s, [])], default=0)
 
-    def size(s):
-        return 1 + sum(size(k) for k in children.get(s, []))
-
-    sides = ("x", "y+", "y-", "z+", "z-")
-    waiting = {side: [] for side in sides}
-    busy = {side: False for side in sides}
-    events = [(0.0, 0, "arrive", (0, 0, 0))]
-    count = 1
+    for kids in children.values():
+        kids.sort(key=lambda s: -depth(s))
+    free = {side: 0.0 for side in ("x", "y+", "y-", "z+", "z-")}
+    events = [(0.0, p, (0, 0, 0), p) for p in range(PIECES)]
+    count = PIECES
     order = []
     while events:
-        now, _, kind, what = heapq.heappop(events)
-        if kind == "free":
-            busy[what] = False
-        else:
-            order.append(what)
-            for k in children.get(what, []):
-                waiting[ARRIVES[k]].append(k)
-        for side in sides:
-            if not busy[side] and waiting[side]:
-                waiting[side].sort(key=lambda s: (-depth(s), -size(s)))
-                s = waiting[side].pop(0)
-                busy[side] = True
-                heapq.heappush(events, (now + wire, count, "free", side))
-                heapq.heappush(
-                    events, (now + wire + (far if side == "x" else hop), count + 1, "arrive", s)
-                )
-                count += 2
-    for kids in children.values():
-        kids.sort(key=lambda s: (-depth(s), -size(s)))
+        now, _, s, p = heapq.heappop(events)
+        order.append((s, p))
+        for kid in children.get(s, []):
+            side = ARRIVES[kid]
+            free[side] = max(free[side], now) + wire
+            heapq.heappush(events, (free[side] + (far if side == "x" else hop), count, kid, p))
+            count += 1
     return order, children
 
 
 ORDER, CHILDREN = gather_order()
-RANK = {s: i for i, s in enumerate(ORDER)}
+RANK = {}
+for _s, _p in ORDER:
+    if _p == PIECES - 1:
+        RANK[_s] = len(RANK)
 
 
 def position_codes():
@@ -142,7 +131,7 @@
     local_sem, send_sem, recv_sem, rep_send, rep_recv, sum_send, sum_recv, out_sem,
 ):
     units = wg.shape[0]
-    width = og.shape[1]
+    width = wg.shape[1]
     part = own.shape[1]
     rep = lax.axis_index("rep")
     me = lax.axis_index("fsdp")
@@ -177,20 +166,24 @@
 
     back = {"x": (1, 0, 0), "y+": (0, -1, 0), "y-": (0, 1, 0), "z+": (0, 0, -1), "z-": (0, 0, 1)}
 
-    def shard_copy(s):
+    def piece_copy(s, p):
         origin = source(s)
         rank = RANK[s]
-        src = tokens_hbm if origin == (0, 0, 0) else x_all.at[pl.ds(RANK[origin] * LEN, LEN), :]
+        lanes = pl.ds(p * (width // PIECES), width // PIECES)
+        if origin == (0, 0, 0):
+            src = tokens_hbm.at[:, lanes]
+        else:
+            src = x_all.at[pl.ds(RANK[origin] * LEN, LEN), lanes]
         return pltpu.make_async_remote_copy(
             src_ref=src,
-            dst_ref=x_all.at[pl.ds(rank * LEN, LEN), :],
-            send_sem=send_sem.at[rank],
-            recv_sem=recv_sem.at[rank],
+            dst_ref=x_all.at[pl.ds(rank * LEN, LEN), lanes],
+            send_sem=send_sem.at[rank * PIECES + p],
+            recv_sem=recv_sem.at[rank * PIECES + p],
             device_id=(rep, at(*back[ARRIVES[s]])),
             device_id_type=MESH,
         )
 
-    copies = {s: shard_copy(s) for s in ARRIVES}
+    copies = {(s, p): piece_copy(s, p) for s in ARRIVES for p in range(PIECES)}
 
     def rep_copy(i, src, dst, distance):
         return pltpu.make_async_remote_copy(
@@ -209,8 +202,9 @@
         rep_copy(5 + d, wg_hbm.at[:, columns(rep ^ d)], slabs.at[d], d) for d in (1, 2, 3)
     ]
 
-    for s in CHILDREN[(0, 0, 0)]:
-        copies[s].start()
+    for p in range(PIECES):
+        for s in CHILDREN[(0, 0, 0)]:
+            copies[s, p].start()
     for copy in (gate_far, gate_near, up_far, up_near, slab_copies[0], slab_copies[1], slab_copies[2]):
         copy.start()
 
@@ -293,11 +287,13 @@
 
     todo = []
     local[0].wait()
-    for rank in range(1, SEQS):
-        s = ORDER[rank]
-        copies[s].wait_recv()
+    for s, p in ORDER[PIECES:]:
+        copies[s, p].wait_recv()
         for child in CHILDREN.get(s, []):
-            copies[child].start()
+            copies[child, p].start()
+        if p < PIECES - 1:
+            continue
+        rank = RANK[s]
         if rank == 20:
             gate_far.wait_recv()
             gate_pass.start()
@@ -398,8 +394,8 @@
         partial = partial + wide[i]
     relative_out[...] = partial
 
-    for s in ORDER[1:]:
-        copies[s].wait_send()
+    for piece in ORDER[PIECES:]:
+        copies[piece].wait_send()
     for copy in (gate_far, up_far, gate_near, up_near, gate_pass, up_pass, *slab_copies):
         copy.wait_send()
     for copy in near_copies + wide_copies:
@@ -445,8 +441,8 @@
             pltpu.VMEM((1, BLOCK), F32),
             pltpu.VMEM((1, BLOCK), F32),
             pltpu.SemaphoreType.DMA((8,)),
-            pltpu.SemaphoreType.DMA((SEQS,)),
-            pltpu.SemaphoreType.DMA((SEQS,)),
+            pltpu.SemaphoreType.DMA((SEQS * PIECES,)),
+            pltpu.SemaphoreType.DMA((SEQS * PIECES,)),
             pltpu.SemaphoreType.DMA((9,)),
             pltpu.SemaphoreType.DMA((9,)),
             pltpu.SemaphoreType.DMA((16,)),

time: 98.4 us -> 91.2 us (0.927)
  Pallas kernels: 97.4 us -> 90.1 us
    pallas_call x1, Pallas kernels: 86.2 us -> 78.8 us  [gather_forward(): pl.pallas_call(gather_kernel, name='gather_forward', out_shape=(jax.Shape...]
where the time goes in v2:
time: 91.2 us; the launch traced here: 90.9 us
  Pallas kernels  90.1 us (99%)
    pallas_call x1, Pallas kernels, gather_forward(): pl.pallas_call(gather_kernel, name='gather_forward', out_shape=(jax.Shape...  78.8 us
    pallas_call x1, Pallas kernels, backward(): pl.pallas_call(backward_kernel, name='backward', grid=(steps,), out_shape...  11.3 us

profile of v2, /device:TPU:2, one launch (start us, length us, event | category | flops | bytes accessed | tf_op | source)
XLA Modules:
  0.0 90.9 jit_solution(5580376631665311747)
XLA Ops:
  0.6 78.8 %gather_forward.1 = (bf16[1024,4096]{1,0:T(8,128)(2,1)}, f32[448,1024]{1,0:T(8,128)}, f32[224,1024]{1,0:T(8,128)}, f32[1,128]{1,0:T(1,128)}) custom-call(s32[1,1024]{1,0:T(1,128)} %constant.2.clone.codes_ref, s32[1,1024]{1,0:T(1,128)} %bitcast.7, bf16[16,4096]{1,0:T(8,128)(2,1)} %tokens_hbm.1, bf16[224,1024]{1,0:T(8,128)(2,1)} %bitcast.6, ...), custom_call_target="tpu_custom_call" | custom-call | tf_op jit(solution)/shard_map/gather_forward/pallas_call | solution.py:414
  79.4 11.3 %backward.1 = (f32[1]{0:T(128)}, bf16[1,224,4096]{2,1,0:T(8,128)(2,1)}, bf16[1,224,4096]{2,1,0:T(8,128)(2,1)}, bf16[224,1024]{1,0:T(8,128)(2,1)}, f32[224,1024]{1,0:T(8,128)}) custom-call(s32[1,1024]{1,0:T(1,128)} %constant.2.clone.codes_ref, s32[1,64]{1,0:T(1,128)} %order_ref.1, f32[1,128]{1,0:T(1,128)} %get-tuple-element.9.relative_ref, ...), custom_call_target="tpu_custom_call" | custom-call | tf_op jit(solution)/shard_map/backward/pallas_call | solution.py:500

commit v3 on v2

v3 whole, which is shorter than its diff:
```python
import functools
import heapq

import jax
import jax.numpy as jnp
import numpy as np
from jax import lax
from jax.experimental import pallas as pl
from jax.experimental.pallas import tpu as pltpu
from jax.sharding import PartitionSpec as P

BLOCK = 128
LEN = 16
NZ, NX, NY = 8, 2, 4
SEQS = NZ * NX * NY
GROUP_TOK = SEQS * LEN
CHUNK = 256
CHUNKS = GROUP_TOK // CHUNK
PER_CHUNK = CHUNK // LEN
PIECES = 2

dpo_beta = 0.1
outer_rate = 0.7
outer_mu = 0.9
tiny_eps = 1e-06

MESH = pl.DeviceIdType.MESH
K1_LIMIT = 20 * 2**20
K2_LIMIT = 16 * 2**20
F32 = jnp.float32
BF16 = jnp.bfloat16


def gather_plan():
    arrives = {}
    flip = 0
    for dx in range(NX):
        for dz in range(NZ):
            for dy in range(NY):
                if (dx, dy, dz) == (0, 0, 0):
                    continue
                if dy == 0 and dz == 0:
                    side = "x"
                elif dz != 0 and (dy == 0 or (dx == 1 and dz != 4)):
                    side = "z+" if dz < 4 or (dz == 4 and dx == 0) else "z-"
                elif dy == 2:
                    side = "y+" if flip % 2 == 0 else "y-"
                    flip += 1
                else:
                    side = "y+" if dy == 1 else "y-"
                for p in range(PIECES):
                    arrives[(dx, dy, dz), p] = side
    for p in range(PIECES // 2):
        arrives[(1, 1, 3), p] = "y+"
        arrives[(1, 3, 5), p] = "y-"
    return arrives


ARRIVES = gather_plan()


def source(s, p):
    dx, dy, dz = s
    side = ARRIVES[s, p]
    if side == "x":
        return (dx ^ 1, dy, dz)
    if side[0] == "y":
        return (dx, (dy + (-1 if side == "y+" else 1)) % NY, dz)
    return (dx, dy, (dz + (-1 if side == "z+" else 1)) % NZ)


def gather_order(wire=2.73 / PIECES, hop=2.2, far=3.0):
    children = {}
    for s, p in ARRIVES:
        children.setdefault((source(s, p), p), []).append((s, p))

    def depth(piece):
        return 1 + max([depth(k) for k in children.get(piece, [])], default=0)

    for kids in children.values():
        kids.sort(key=lambda piece: -depth(piece))
    free = {side: 0.0 for side in ("x", "y+", "y-", "z+", "z-")}
    events = [(0.0, p, ((0, 0, 0), p)) for p in range(PIECES)]
    count = PIECES
    order = []
    while events:
        now, _, piece = heapq.heappop(events)
        order.append(piece)
        for kid in children.get(piece, []):
            side = ARRIVES[kid]
            free[side] = max(free[side], now) + wire
            heapq.heappush(events, (free[side] + (far if side == "x" else hop), count, kid))
            count += 1
    return order, children


ORDER, CHILDREN = gather_order()
RANK = {}
for _i, (_s, _) in enumerate(ORDER):
    if all(_s != later for later, _ in ORDER[_i + 1:]):
        RANK[_s] = len(RANK)


def position_codes():
    codes = np.zeros((1, GROUP_TOK), np.int32)
    for (dx, dy, dz), rank in RANK.items():
        codes[0, rank * LEN:(rank + 1) * LEN] = dz * 8 + dx * 4 + dy
    return codes


def sequence_of(codes):
    me = lax.axis_index("fsdp")
    z, x, y = me // 8, (me // 4) % 2, me % 4
    dz, dx, dy = codes >> 3, (codes >> 2) & 1, codes & 3
    return (((dz + z) & 7) << 3) + (((dx + x) & 1) << 2) + ((dy + y) & 3)


def iota(shape, axis):
    return lax.broadcasted_iota(jnp.int32, shape, axis)


def column_to_row(column, rows, lanes):
    eye = iota((rows, lanes), 0) == iota((rows, lanes), 1)
    return jnp.sum(jnp.where(eye, column, 0.0), axis=0, keepdims=True)


def row_to_column(row, rows, lanes):
    eye = iota((rows, lanes), 0) == iota((rows, lanes), 1)
    return jnp.sum(jnp.where(eye, row, 0.0), axis=1, keepdims=True)


def gather_kernel(
    codes_hbm, mask_hbm, tokens_hbm, readout_hbm, wg_hbm, wu_hbm, og_hbm, ou_hbm,
    x_all, grads, average, relative_out,
    codes_ref, mask_ref, policy, outer, own, slabs, readout, both, token_score,
    near, wide, near_own, wide_own,
    local_sem, send_sem, recv_sem, rep_send, rep_recv, sum_send, sum_recv,
):
    units, width = wg_hbm.shape
    part = own.shape[1]
    rep = lax.axis_index("rep")
    me = lax.axis_index("fsdp")
    z, x, y = me // 8, (me // 4) % 2, me % 4

    def at(dx, dy, dz):
        return ((z + dz) % 8) * 8 + ((x + dx) % 2) * 4 + (y + dy) % 4

    barrier = pltpu.get_barrier_semaphore()
    peers = [(rep, at(0, 0, d)) for d in range(1, NZ)]
    peers += [(rep, at(d // 4, d % 4, 0)) for d in range(1, NX * NY)]
    peers += [(rep ^ d, me) for d in range(1, 4)]
    for peer in peers:
        pl.semaphore_signal(barrier, inc=1, device_id=peer, device_id_type=MESH)

    def columns(r):
        return pl.ds(pl.multiple_of(r * part, part), part)

    local = [
        pltpu.make_async_copy(tokens_hbm, x_all.at[pl.ds(0, LEN), :], local_sem.at[0]),
        pltpu.make_async_copy(readout_hbm, readout, local_sem.at[1]),
        pltpu.make_async_copy(wg_hbm, policy.at[pl.ds(0, units), :], local_sem.at[2]),
        pltpu.make_async_copy(wu_hbm, policy.at[pl.ds(units, units), :], local_sem.at[3]),
        pltpu.make_async_copy(og_hbm, own, local_sem.at[4]),
        pltpu.make_async_copy(og_hbm, outer.at[pl.ds(0, units), columns(rep)], local_sem.at[5]),
        pltpu.make_async_copy(ou_hbm, outer.at[pl.ds(units, units), columns(rep)], local_sem.at[6]),
        pltpu.make_async_copy(wg_hbm.at[:, columns(rep)], slabs.at[0], local_sem.at[7]),
        pltpu.make_async_copy(codes_hbm, codes_ref, local_sem.at[8]),
        pltpu.make_async_copy(mask_hbm, mask_ref, local_sem.at[9]),
    ]
    for copy in local:
        copy.start()
    pl.semaphore_wait(barrier, len(peers))

    back = {"x": (1, 0, 0), "y+": (0, -1, 0), "y-": (0, 1, 0), "z+": (0, 0, -1), "z-": (0, 0, 1)}

    def piece_copy(s, p):
        origin = source(s, p)
        rank = RANK[s]
        lanes = pl.ds(p * (width // PIECES), width // PIECES)
        if origin == (0, 0, 0):
            src = tokens_hbm.at[:, lanes]
        else:
            src = x_all.at[pl.ds(RANK[origin] * LEN, LEN), lanes]
        return pltpu.make_async_remote_copy(
            src_ref=src,
            dst_ref=x_all.at[pl.ds(rank * LEN, LEN), lanes],
            send_sem=send_sem.at[rank * PIECES + p],
            recv_sem=recv_sem.at[rank * PIECES + p],
            device_id=(rep, at(*back[ARRIVES[s, p]])),
            device_id_type=MESH,
        )

    copies = {(s, p): piece_copy(s, p) for s, p in ARRIVES}

    def rep_copy(i, src, dst, distance):
        return pltpu.make_async_remote_copy(
            src_ref=src, dst_ref=dst, send_sem=rep_send.at[i], recv_sem=rep_recv.at[i],
            device_id=(rep ^ distance, me), device_id_type=MESH,
        )

    gate_rows, up_rows = pl.ds(0, units), pl.ds(units, units)
    mine, across = columns(rep), columns(rep ^ 2)
    gate_far = rep_copy(0, og_hbm, outer.at[gate_rows, mine], 2)
    up_far = rep_copy(1, ou_hbm, outer.at[up_rows, mine], 2)
    gate_near = rep_copy(2, og_hbm, outer.at[gate_rows, mine], 1)
    up_near = rep_copy(3, ou_hbm, outer.at[up_rows, mine], 1)
    gate_pass = rep_copy(4, outer.at[gate_rows, across], outer.at[gate_rows, across], 1)
    up_pass = rep_copy(5, outer.at[up_rows, across], outer.at[up_rows, across], 1)
    slab_copies = [
        rep_copy(5 + d, wg_hbm.at[:, columns(rep ^ d)], slabs.at[d], d) for d in (1, 2, 3)
    ]

    for p in range(PIECES):
        for piece in CHILDREN[(0, 0, 0), p]:
            copies[piece].start()
    for copy in (gate_far, gate_near, up_far, up_near, slab_copies[0], slab_copies[1], slab_copies[2]):
        copy.start()

    for i in (1, 8, 9):
        local[i].wait()
    masked = (readout[...].astype(F32) * mask_ref[...].astype(F32)).astype(BF16)
    sequence = sequence_of(codes_ref[...])
    wanted = sequence * LEN + (iota((1, GROUP_TOK), 1) & (LEN - 1))
    for c in range(CHUNKS):
        lanes = slice(c * CHUNK, (c + 1) * CHUNK)
        pick = (iota((GROUP_TOK, CHUNK), 0) == wanted[:, lanes]).astype(F32).astype(BF16)
        readout[:, lanes] = jnp.dot(masked, pick, preferred_element_type=F32).astype(BF16)
    token_score[...] = jnp.zeros_like(token_score)
    for i in (2, 3):
        local[i].wait()

    ROWS = 32
    HALF = width // 2

    def unit_project(weights, c, half):
        cols = pl.ds(half * HALF, HALF)
        product = lax.dot_general(
            weights[:, cols], x_all[pl.ds(c * CHUNK, CHUNK), cols], (((1,), (1,)), ((), ())),
            preferred_element_type=F32,
        )
        if half == 0:
            both[...] = product
        else:
            both[...] += product

    def unit_policy(c):
        lanes = pl.ds(c * CHUNK, CHUNK)

        def body(i, total):
            rows = pl.ds(pl.multiple_of(i * ROWS, ROWS), ROWS)
            upper_rows = pl.ds(pl.multiple_of(units + i * ROWS, ROWS), ROWS)
            gate, upper = both[rows, :], both[upper_rows, :]
            read = readout[rows, lanes].astype(F32)
            sigma = jax.nn.sigmoid(gate)
            silu = gate * sigma
            hidden = (silu * upper).astype(BF16).astype(F32)
            grads[rows, lanes] = read * upper * sigma * (1.0 + gate * (1.0 - sigma))
            grads[upper_rows, lanes] = read * silu
            return total + jnp.sum(hidden * read, axis=0, keepdims=True)

        total = lax.fori_loop(0, units // ROWS, body, jnp.zeros((1, CHUNK), F32))
        token_score[:, lanes] += total

    def unit_reference(c):
        lanes = pl.ds(c * CHUNK, CHUNK)

        def body(i, total):
            rows = pl.ds(pl.multiple_of(i * ROWS, ROWS), ROWS)
            upper_rows = pl.ds(pl.multiple_of(units + i * ROWS, ROWS), ROWS)
            gate, upper = both[rows, :], both[upper_rows, :]
            read = readout[rows, lanes].astype(F32)
            hidden = (gate * jax.nn.sigmoid(gate) * upper).astype(BF16).astype(F32)
            return total + jnp.sum(hidden * read, axis=0, keepdims=True)

        total = lax.fori_loop(0, units // ROWS, body, jnp.zeros((1, CHUNK), F32))
        token_score[:, lanes] -= total

    def policy_units(c):
        return [
            functools.partial(unit_project, policy, c, 0),
            functools.partial(unit_project, policy, c, 1),
            functools.partial(unit_policy, c),
        ]

    def reference_units(c):
        return [
            functools.partial(unit_project, outer, c, 0),
            functools.partial(unit_project, outer, c, 1),
            functools.partial(unit_reference, c),
        ]

    todo = []
    local[0].wait()
    left = {s: PIECES for s in RANK}
    for s, p in ORDER[PIECES:]:
        copies[s, p].wait_recv()
        for piece in CHILDREN.get((s, p), []):
            copies[piece].start()
        left[s] -= 1
        if left[s]:
            continue
        rank = RANK[s]
        if rank == 20:
            gate_far.wait_recv()
            gate_pass.start()
        if rank == 36:
            up_far.wait_recv()
            up_pass.start()
        if rank == 40:
            local[5].wait()
            local[6].wait()
            for copy in (gate_near, up_near, gate_pass, up_pass):
                copy.wait_recv()
            todo += reference_units(0) + reference_units(1)
        if rank % PER_CHUNK == PER_CHUNK - 1:
            c = rank // PER_CHUNK
            todo += policy_units(c)
            if c >= 2:
                todo += reference_units(c)
        if todo:
            todo.pop(0)()
    for unit in todo:
        unit()

    belongs = iota((SEQS, GROUP_TOK), 0) == sequence
    partial = jnp.sum(jnp.where(belongs, token_score[...], 0.0), axis=1, keepdims=True)
    partial = column_to_row(partial, SEQS, BLOCK)
    near_own[...] = partial
    near_copies = [
        pltpu.make_async_remote_copy(
            src_ref=near_own, dst_ref=near.at[z], send_sem=sum_send.at[d], recv_sem=sum_recv.at[z],
            device_id=(rep, at(0, 0, d)), device_id_type=MESH,
        )
        for d in (4, 3, 5, 2, 6, 1, 7)
    ]
    for copy in near_copies:
        copy.start()
    near[z] = partial

    for copy in slab_copies:
        copy.wait_recv()
    local[4].wait()
    local[7].wait()
    STEP = 16

    def pseudo(i, _):
        rows = pl.ds(pl.multiple_of(i * STEP, STEP), STEP)
        for b in range(part // BLOCK):
            lanes = slice(b * BLOCK, (b + 1) * BLOCK)
            own_block = own[rows, lanes].astype(F32)
            total = jnp.zeros((STEP, BLOCK), F32)
            for r in range(4):
                delta = own_block - slabs[r, rows, lanes].astype(F32)
                scale = jnp.max(jnp.abs(delta), axis=1, keepdims=True) + tiny_eps
                scale = scale.astype(BF16).astype(F32)
                total += (delta / scale).astype(BF16).astype(F32) * scale
            average[rows, lanes] = total * 0.25
        return 0

    half = units // STEP // 2
    lax.fori_loop(0, half, pseudo, 0)

    for d in range(1, NZ):
        pltpu.make_async_remote_copy(
            src_ref=near_own, dst_ref=near.at[(z + d) % 8], send_sem=sum_send.at[d],
            recv_sem=sum_recv.at[(z + d) % 8], device_id=(rep, at(0, 0, d)), device_id_type=MESH,
        ).wait_recv()
    partial = near[0]
    for i in range(1, NZ):
        partial = partial + near[i]
    plane = x * 4 + y
    wide_own[...] = partial
    wide_copies = [
        pltpu.make_async_remote_copy(
            src_ref=wide_own, dst_ref=wide.at[plane], send_sem=sum_send.at[8 + d],
            recv_sem=sum_recv.at[8 + plane], device_id=(rep, at(d // 4, d % 4, 0)), device_id_type=MESH,
        )
        for d in (6, 5, 7, 2, 4, 1, 3)
    ]
    for copy in wide_copies:
        copy.start()
    wide[plane] = partial

    lax.fori_loop(half, units // STEP, pseudo, 0)

    for d in range(1, NX * NY):
        other = ((x + d // 4) % 2) * 4 + (y + d % 4) % 4
        pltpu.make_async_remote_copy(
            src_ref=wide_own, dst_ref=wide.at[other], send_sem=sum_send.at[8 + d],
            recv_sem=sum_recv.at[8 + other], device_id=(rep, at(d // 4, d % 4, 0)), device_id_type=MESH,
        ).wait_recv()
    partial = wide[0]
    for i in range(1, NX * NY):
        partial = partial + wide[i]
    relative_out[...] = partial

    for piece in ORDER[PIECES:]:
        copies[piece].wait_send()
    for copy in (gate_far, up_far, gate_near, up_near, gate_pass, up_pass, *slab_copies):
        copy.wait_send()
    for copy in near_copies + wide_copies:
        copy.wait_send()


def gather_forward(codes, mask, tokens, readout_t, w_gate, w_up, outer_gate, outer_up):
    units, width = w_gate.shape
    part = outer_gate.shape[1]
    vmem_spec = pl.BlockSpec(memory_space=pltpu.VMEM)
    return pl.pallas_call(
        gather_kernel,
        name="gather_forward",
        out_shape=(
            jax.ShapeDtypeStruct((GROUP_TOK, width), BF16),
            jax.ShapeDtypeStruct((2 * units, GROUP_TOK), F32),
            jax.ShapeDtypeStruct((units, part), F32),
            jax.ShapeDtypeStruct((1, BLOCK), F32),
        ),
        in_specs=[pl.BlockSpec(memory_space=pltpu.HBM)] * 8,
        out_specs=(vmem_spec,) * 4,
        scratch_shapes=[
            pltpu.VMEM((1, GROUP_TOK), jnp.int32),
            pltpu.VMEM((1, GROUP_TOK), jnp.int32),
            pltpu.VMEM((2 * units, width), BF16),
            pltpu.VMEM((2 * units, width), BF16),
            pltpu.VMEM((units, part), BF16),
            pltpu.VMEM((4, units, part), BF16),
            pltpu.VMEM((units, GROUP_TOK), BF16),
            pltpu.VMEM((2 * units, CHUNK), F32),
            pltpu.VMEM((1, GROUP_TOK), F32),
            pltpu.VMEM((NZ, 1, BLOCK), F32),
            pltpu.VMEM((NX * NY, 1, BLOCK), F32),
            pltpu.VMEM((1, BLOCK), F32),
            pltpu.VMEM((1, BLOCK), F32),
            pltpu.SemaphoreType.DMA((10,)),
            pltpu.SemaphoreType.DMA((SEQS * PIECES,)),
            pltpu.SemaphoreType.DMA((SEQS * PIECES,)),
            pltpu.SemaphoreType.DMA((9,)),
            pltpu.SemaphoreType.DMA((9,)),
            pltpu.SemaphoreType.DMA((16,)),
            pltpu.SemaphoreType.DMA((16,)),
        ],
        compiler_params=pltpu.CompilerParams(
            collective_id=0, has_side_effects=True, vmem_limit_bytes=K1_LIMIT
        ),
    )(*(pltpu.with_memory_space_constraint(a, pltpu.HBM) for a in (
        codes, mask, tokens, readout_t, w_gate, w_up, outer_gate, outer_up
    )))


STEPS = 8


def backward_kernel(
    codes_ref, order_ref, relative_ref, grads, x_all, average, outer, moment,
    loss_out, gate_hbm, up_hbm, new_outer_hbm, new_moment_hbm,
    scaled, products, new_outer, new_moment, state_sem, out_sem,
):
    units = outer.shape[0]
    width = x_all.shape[1]
    block, slab = width // STEPS, outer.shape[1] // STEPS
    pairs = SEQS // 2

    relative = row_to_column(relative_ref[...], SEQS, BLOCK)
    placed = iota((SEQS, SEQS), 0) == order_ref[...]
    by_place = jnp.sum(jnp.where(placed, relative, 0.0), axis=0, keepdims=True)
    place, pair = iota((pairs, SEQS), 1), iota((pairs, SEQS), 0)
    sign = jnp.where(place == 2 * pair, 1.0, jnp.where(place == 2 * pair + 1, -1.0, 0.0))
    margin = dpo_beta * jnp.sum(sign * by_place, axis=1, keepdims=True)
    loss_out[0] = jnp.sum(jax.nn.softplus(-margin)) / pairs
    weight = dpo_beta * jax.nn.sigmoid(-margin) / pairs
    place_coef = jnp.sum(-sign * weight, axis=0, keepdims=True)
    coef = jnp.sum(jnp.where(placed, place_coef, 0.0), axis=1, keepdims=True)
    belongs = iota((SEQS, GROUP_TOK), 0) == sequence_of(codes_ref[...])
    token_grad = jnp.sum(jnp.where(belongs, coef, 0.0), axis=0, keepdims=True)
    scaled[...] = (grads[...] * token_grad).astype(BF16)

    out_copies = []
    for i in range(STEPS):
        cols = pl.ds(i * block, block)
        products[:, cols] = jnp.dot(
            scaled[...], x_all[:, cols], preferred_element_type=F32
        ).astype(BF16)
        lanes = slice(i * slab, (i + 1) * slab)
        fresh = outer_mu * moment[:, lanes] + average[:, lanes]
        new_moment[:, lanes] = fresh
        new_outer[:, lanes] = (
            outer[:, lanes].astype(F32) - outer_rate * (average[:, lanes] + outer_mu * fresh)
        ).astype(BF16)
        out_copies += [
            pltpu.make_async_copy(
                products.at[pl.ds(0, units), cols], gate_hbm.at[0, :, cols], out_sem.at[2 * i]
            ),
            pltpu.make_async_copy(
                products.at[pl.ds(units, units), cols], up_hbm.at[0, :, cols], out_sem.at[2 * i + 1]
            ),
        ]
        out_copies[-2].start()
        out_copies[-1].start()
    out_copies += [
        pltpu.make_async_copy(new_outer, new_outer_hbm, state_sem.at[0]),
        pltpu.make_async_copy(new_moment, new_moment_hbm, state_sem.at[1]),
    ]
    out_copies[-2].start()
    out_copies[-1].start()
    for copy in out_copies:
        copy.wait()


def backward(codes, order, relative, grads, x_all, average, outer_gate, moment):
    units, part = outer_gate.shape
    width = x_all.shape[1]
    any_spec = pl.BlockSpec(memory_space=pl.ANY)
    vmem_spec = pl.BlockSpec(memory_space=pltpu.VMEM)
    return pl.pallas_call(
        backward_kernel,
        name="backward",
        out_shape=(
            jax.ShapeDtypeStruct((1,), F32),
            jax.ShapeDtypeStruct((1, units, width), BF16),
            jax.ShapeDtypeStruct((1, units, width), BF16),
            jax.ShapeDtypeStruct((units, part), BF16),
            jax.ShapeDtypeStruct((units, part), F32),
        ),
        in_specs=[vmem_spec] * 8,
        out_specs=(pl.BlockSpec(memory_space=pltpu.SMEM),) + (any_spec,) * 4,
        scratch_shapes=[
            pltpu.VMEM((2 * units, GROUP_TOK), BF16),
            pltpu.VMEM((2 * units, width), BF16),
            pltpu.VMEM((units, part), BF16),
            pltpu.VMEM((units, part), F32),
            pltpu.SemaphoreType.DMA((2,)),
            pltpu.SemaphoreType.DMA((2 * STEPS,)),
        ],
        compiler_params=pltpu.CompilerParams(vmem_limit_bytes=K2_LIMIT),
    )(codes, order, relative, grads, x_all, average, outer_gate, moment)


def per_device(tokens, readout, resp_mask, order, w_gate, w_up, outer_gate, outer_up, moment):
    codes = jnp.asarray(position_codes())
    x_all, grads, average, relative = gather_forward(
        codes, resp_mask.reshape(1, -1), tokens, readout.T, w_gate[0], w_up[0], outer_gate, outer_up
    )
    return backward(codes, order, relative, grads, x_all, average, outer_gate, moment)


def solution(mesh):
    return jax.shard_map(
        per_device,
        mesh=mesh,
        in_specs=(
            P(("rep", "fsdp"), None),
            P("rep", "fsdp"),
            P("rep"),
            P("rep", None),
            P("rep", "fsdp", None),
            P("rep", "fsdp", None),
            P("fsdp", "rep"),
            P("fsdp", "rep"),
            P("fsdp", "rep"),
        ),
        out_specs=(
            P("rep"),
            P("rep", "fsdp", None),
            P("rep", "fsdp", None),
            P("fsdp", "rep"),
            P("fsdp", "rep"),
        ),
        check_vma=False,
    )
```

time: 91.2 us -> 83.1 us (0.911)
  Pallas kernels: 90.1 us -> 82.1 us
    pallas_call x1, Pallas kernels: 11.3 us -> 6.46 us  [backward(): pl.pallas_call(backward_kernel, name='backward', out_shape=(jax.ShapeDtyp...]
    pallas_call x1, Pallas kernels: 78.8 us -> 75.6 us  [gather_forward(): pl.pallas_call(gather_kernel, name='gather_forward', out_shape=(jax.Shape...]
where the time goes in v3:
time: 83.1 us; the launch traced here: 83 us
  Pallas kernels  82.1 us (99%)
  between operations  0.87 us (1%)
    pallas_call x1, Pallas kernels, gather_forward(): pl.pallas_call(gather_kernel, name='gather_forward', out_shape=(jax.Shape...  75.6 us
    pallas_call x1, Pallas kernels, backward(): pl.pallas_call(backward_kernel, name='backward', out_shape=(jax.ShapeDtyp...  6.46 us

profile of v3, /device:TPU:2, one launch (start us, length us, event | category | flops | bytes accessed | tf_op | source)
XLA Modules:
  0.0 83.0 jit_solution(5404780777558759190)
XLA Ops:
  0.6 0.0 copy-start
  0.6 0.0 copy-start.1
  0.7 0.0 copy-start.2
  0.7 0.0 copy-start.3
  0.7 75.6 %gather_forward.1 = (bf16[1024,4096]{1,0:T(8,128)(2,1)S(1)}, f32[448,1024]{1,0:T(8,128)S(1)}, f32[224,1024]{1,0:T(8,128)S(1)}, f32[1,128]{1,0:T(1,128)S(1)}) custom-call(s32[1,1024]{1,0:T(1,128)} %constant.2.clone.codes_hbm.codes_ref, s32[1,1024]{1,0:T(1,128)} %bitcast.7, bf16[16,4096]{1,0:T(8,128)(2,1)} %tokens_hbm.1, bf16[224,1024]{1,0:T(8,128)(2,1)} %bitcast.6, ...), custom_call_target="tpu_custom_call" | custom-call | tf_op jit(solution)/shard_map/gather_forward/pallas_call | solution.py:409
  76.3 0.0 copy-done
  76.3 0.0 copy-done.1
  76.3 0.0 copy-done.2
  76.4 0.0 copy-done.3
  76.4 6.5 %backward.1 = (f32[1]{0:T(128)}, bf16[1,224,4096]{2,1,0:T(8,128)(2,1)}, bf16[1,224,4096]{2,1,0:T(8,128)(2,1)}, bf16[224,1024]{1,0:T(8,128)(2,1)}, f32[224,1024]{1,0:T(8,128)}) custom-call(s32[1,1024]{1,0:T(1,128)S(1)} %copy-done.2, s32[1,64]{1,0:T(1,128)S(1)} %copy-done.3, f32[1,128]{1,0:T(1,128)S(1)} %get-tuple-element.9.relative_ref, ...), custom_call_target="tpu_custom_call" | custom-call | tf_op jit(solution)/shard_map/backward/pallas_call | solution.py:514
Async XLA Ops:
  0.6 75.7 %copy-start = (bf16[224,1024]{1,0:T(8,128)(2,1)S(1)}, bf16[224,1024]{1,0:T(8,128)(2,1)}, u32[]{:S(2)}) copy-start(bf16[224,1024]{1,0:T(8,128)(2,1)} %outer.1) | copy-start | bytes 1376260
  0.6 75.7 %copy-start.1 = (f32[224,1024]{1,0:T(8,128)S(1)}, f32[224,1024]{1,0:T(8,128)}, u32[]{:S(2)}) copy-start(f32[224,1024]{1,0:T(8,128)} %moment.1) | copy-start | bytes 2752516
  0.7 75.7 %copy-start.2 = (s32[1,1024]{1,0:T(1,128)S(1)}, s32[1,1024]{1,0:T(1,128)}, u32[]{:S(2)}) copy-start(s32[1,1024]{1,0:T(1,128)} %constant.2.clone.codes_hbm.codes_ref) | copy-start | bytes 12292
  0.7 75.7 %copy-start.3 = (s32[1,64]{1,0:T(1,128)S(1)}, s32[1,64]{1,0:T(1,128)}, u32[]{:S(2)}) copy-start(s32[1,64]{1,0:T(1,128)} %order_ref.1) | copy-start | bytes 772

commit v4 on v3

--- a/solution.py
+++ b/solution.py
@@ -14,9 +14,7 @@
 NZ, NX, NY = 8, 2, 4
 SEQS = NZ * NX * NY
 GROUP_TOK = SEQS * LEN
-CHUNK = 256
-CHUNKS = GROUP_TOK // CHUNK
-PER_CHUNK = CHUNK // LEN
+CHUNKS = ((0, 256), (256, 256), (512, 256), (768, 128), (896, 128))
 PIECES = 2
 
 dpo_beta = 0.1
@@ -146,8 +144,7 @@
         return ((z + dz) % 8) * 8 + ((x + dx) % 2) * 4 + (y + dy) % 4
 
     barrier = pltpu.get_barrier_semaphore()
-    peers = [(rep, at(0, 0, d)) for d in range(1, NZ)]
-    peers += [(rep, at(d // 4, d % 4, 0)) for d in range(1, NX * NY)]
+    peers = [(rep, at(*side)) for side in ((0, 0, 1), (0, 0, -1), (0, 1, 0), (0, -1, 0), (1, 0, 0))]
     peers += [(rep ^ d, me) for d in range(1, 4)]
     for peer in peers:
         pl.semaphore_signal(barrier, inc=1, device_id=peer, device_id_type=MESH)
@@ -221,35 +218,31 @@
     masked = (readout[...].astype(F32) * mask_ref[...].astype(F32)).astype(BF16)
     sequence = sequence_of(codes_ref[...])
     wanted = sequence * LEN + (iota((1, GROUP_TOK), 1) & (LEN - 1))
-    for c in range(CHUNKS):
-        lanes = slice(c * CHUNK, (c + 1) * CHUNK)
-        pick = (iota((GROUP_TOK, CHUNK), 0) == wanted[:, lanes]).astype(F32).astype(BF16)
+    for start in range(0, GROUP_TOK, 256):
+        lanes = slice(start, start + 256)
+        pick = (iota((GROUP_TOK, 256), 0) == wanted[:, lanes]).astype(F32).astype(BF16)
         readout[:, lanes] = jnp.dot(masked, pick, preferred_element_type=F32).astype(BF16)
     token_score[...] = jnp.zeros_like(token_score)
     for i in (2, 3):
         local[i].wait()
 
     ROWS = 32
-    HALF = width // 2
-
-    def unit_project(weights, c, half):
-        cols = pl.ds(half * HALF, HALF)
-        product = lax.dot_general(
-            weights[:, cols], x_all[pl.ds(c * CHUNK, CHUNK), cols], (((1,), (1,)), ((), ())),
+
+    def unit_project(weights, rows, c):
+        start, size = CHUNKS[c]
+        both[rows, pl.ds(0, size)] = lax.dot_general(
+            weights[rows, :], x_all[pl.ds(start, size), :], (((1,), (1,)), ((), ())),
             preferred_element_type=F32,
         )
-        if half == 0:
-            both[...] = product
-        else:
-            both[...] += product
 
     def unit_policy(c):
-        lanes = pl.ds(c * CHUNK, CHUNK)
+        start, size = CHUNKS[c]
+        lanes, used = pl.ds(start, size), pl.ds(0, size)
 
         def body(i, total):
             rows = pl.ds(pl.multiple_of(i * ROWS, ROWS), ROWS)
             upper_rows = pl.ds(pl.multiple_of(units + i * ROWS, ROWS), ROWS)
-            gate, upper = both[rows, :], both[upper_rows, :]
+            gate, upper = both[rows, used], both[upper_rows, used]
             read = readout[rows, lanes].astype(F32)
             sigma = jax.nn.sigmoid(gate)
             silu = gate * sigma
@@ -258,34 +251,35 @@
             grads[upper_rows, lanes] = read * silu
             return total + jnp.sum(hidden * read, axis=0, keepdims=True)
 
-        total = lax.fori_loop(0, units // ROWS, body, jnp.zeros((1, CHUNK), F32))
+        total = lax.fori_loop(0, units // ROWS, body, jnp.zeros((1, size), F32))
         token_score[:, lanes] += total
 
     def unit_reference(c):
-        lanes = pl.ds(c * CHUNK, CHUNK)
+        start, size = CHUNKS[c]
+        lanes, used = pl.ds(start, size), pl.ds(0, size)
 
         def body(i, total):
             rows = pl.ds(pl.multiple_of(i * ROWS, ROWS), ROWS)
             upper_rows = pl.ds(pl.multiple_of(units + i * ROWS, ROWS), ROWS)
-            gate, upper = both[rows, :], both[upper_rows, :]
+            gate, upper = both[rows, used], both[upper_rows, used]
             read = readout[rows, lanes].astype(F32)
             hidden = (gate * jax.nn.sigmoid(gate) * upper).astype(BF16).astype(F32)
             return total + jnp.sum(hidden * read, axis=0, keepdims=True)
 
-        total = lax.fori_loop(0, units // ROWS, body, jnp.zeros((1, CHUNK), F32))
+        total = lax.fori_loop(0, units // ROWS, body, jnp.zeros((1, size), F32))
         token_score[:, lanes] -= total
 
     def policy_units(c):
         return [
-            functools.partial(unit_project, policy, c, 0),
-            functools.partial(unit_project, policy, c, 1),
+            functools.partial(unit_project, policy, gate_rows, c),
+            functools.partial(unit_project, policy, up_rows, c),
             functools.partial(unit_policy, c),
         ]
 
     def reference_units(c):
         return [
-            functools.partial(unit_project, outer, c, 0),
-            functools.partial(unit_project, outer, c, 1),
+            functools.partial(unit_project, outer, gate_rows, c),
+            functools.partial(unit_project, outer, up_rows, c),
             functools.partial(unit_reference, c),
         ]
 
@@ -300,20 +294,21 @@
         if left[s]:
             continue
         rank = RANK[s]
-        if rank == 20:
+        if rank == 19:
             gate_far.wait_recv()
             gate_pass.start()
-        if rank == 36:
+        if rank == 33:
             up_far.wait_recv()
             up_pass.start()
-        if rank == 40:
+        if rank == 37:
             local[5].wait()
             local[6].wait()
             for copy in (gate_near, up_near, gate_pass, up_pass):
                 copy.wait_recv()
             todo += reference_units(0) + reference_units(1)
-        if rank % PER_CHUNK == PER_CHUNK - 1:
-            c = rank // PER_CHUNK
+        for c, (start, size) in enumerate(CHUNKS):
+            if (rank + 1) * LEN != start + size:
+                continue
             todo += policy_units(c)
             if c >= 2:
                 todo += reference_units(c)
@@ -425,7 +420,7 @@
             pltpu.VMEM((units, part), BF16),
             pltpu.VMEM((4, units, part), BF16),
             pltpu.VMEM((units, GROUP_TOK), BF16),
-            pltpu.VMEM((2 * units, CHUNK), F32),
+            pltpu.VMEM((2 * units, 256), F32),
             pltpu.VMEM((1, GROUP_TOK), F32),
             pltpu.VMEM((NZ, 1, BLOCK), F32),
             pltpu.VMEM((NX * NY, 1, BLOCK), F32),

time: 83.1 us -> 80.6 us (0.970)
  Pallas kernels: 82.1 us -> 79.5 us
    pallas_call x1, Pallas kernels: 75.6 us -> 73 us  [gather_forward(): pl.pallas_call(gather_kernel, name='gather_forward', out_shape=(jax.Shape...]
where the time goes in v4:
time: 80.6 us; the launch traced here: 80.4 us
  Pallas kernels  79.5 us (99%)
  between operations  0.89 us (1%)
    pallas_call x1, Pallas kernels, gather_forward(): pl.pallas_call(gather_kernel, name='gather_forward', out_shape=(jax.Shape...  73 us
    pallas_call x1, Pallas kernels, backward(): pl.pallas_call(backward_kernel, name='backward', out_shape=(jax.ShapeDtyp...  6.46 us

profile of v4, /device:TPU:2, one launch (start us, length us, event | category | flops | bytes accessed | tf_op | source)
XLA Modules:
  0.0 80.4 jit_solution(16310175575269872807)
XLA Ops:
  0.6 0.0 copy-start
  0.6 0.0 copy-start.1
  0.7 0.0 copy-start.2
  0.7 0.0 copy-start.3
  0.7 73.0 %gather_forward.1 = (bf16[1024,4096]{1,0:T(8,128)(2,1)S(1)}, f32[448,1024]{1,0:T(8,128)S(1)}, f32[224,1024]{1,0:T(8,128)S(1)}, f32[1,128]{1,0:T(1,128)S(1)}) custom-call(s32[1,1024]{1,0:T(1,128)} %constant.2.clone.codes_hbm.codes_ref, s32[1,1024]{1,0:T(1,128)} %bitcast.7, bf16[16,4096]{1,0:T(8,128)(2,1)} %tokens_hbm.1, bf16[224,1024]{1,0:T(8,128)(2,1)} %bitcast.6, ...), custom_call_target="tpu_custom_call" | custom-call | tf_op jit(solution)/shard_map/gather_forward/pallas_call | solution.py:404
  73.7 0.0 copy-done
  73.7 0.0 copy-done.1
  73.7 0.0 copy-done.2
  73.7 0.0 copy-done.3
  73.7 6.5 %backward.1 = (f32[1]{0:T(128)}, bf16[1,224,4096]{2,1,0:T(8,128)(2,1)}, bf16[1,224,4096]{2,1,0:T(8,128)(2,1)}, bf16[224,1024]{1,0:T(8,128)(2,1)}, f32[224,1024]{1,0:T(8,128)}) custom-call(s32[1,1024]{1,0:T(1,128)S(1)} %copy-done.2, s32[1,64]{1,0:T(1,128)S(1)} %copy-done.3, f32[1,128]{1,0:T(1,128)S(1)} %get-tuple-element.9.relative_ref, ...), custom_call_target="tpu_custom_call" | custom-call | tf_op jit(solution)/shard_map/backward/pallas_call | solution.py:509
Async XLA Ops:
  0.6 73.1 %copy-start = (bf16[224,1024]{1,0:T(8,128)(2,1)S(1)}, bf16[224,1024]{1,0:T(8,128)(2,1)}, u32[]{:S(2)}) copy-start(bf16[224,1024]{1,0:T(8,128)(2,1)} %outer.1) | copy-start | bytes 1376260
  0.6 73.1 %copy-start.1 = (f32[224,1024]{1,0:T(8,128)S(1)}, f32[224,1024]{1,0:T(8,128)}, u32[]{:S(2)}) copy-start(f32[224,1024]{1,0:T(8,128)} %moment.1) | copy-start | bytes 2752516
  0.7 73.1 %copy-start.2 = (s32[1,1024]{1,0:T(1,128)S(1)}, s32[1,1024]{1,0:T(1,128)}, u32[]{:S(2)}) copy-start(s32[1,1024]{1,0:T(1,128)} %constant.2.clone.codes_hbm.codes_ref) | copy-start | bytes 12292
  0.7 73.1 %copy-start.3 = (s32[1,64]{1,0:T(1,128)S(1)}, s32[1,64]{1,0:T(1,128)}, u32[]{:S(2)}) copy-start(s32[1,64]{1,0:T(1,128)} %order_ref.1) | copy-start | bytes 772

commit v5 on v4

--- a/solution.py
+++ b/solution.py
@@ -130,8 +130,8 @@
 def gather_kernel(
     codes_hbm, mask_hbm, tokens_hbm, readout_hbm, wg_hbm, wu_hbm, og_hbm, ou_hbm,
     x_all, grads, average, relative_out,
-    codes_ref, mask_ref, policy, outer, own, slabs, readout, both, token_score,
-    near, wide, near_own, wide_own,
+    codes_ref, mask_ref, policy, outer, own, slabs, readout, masked, both, token_score,
+    scores, own_score,
     local_sem, send_sem, recv_sem, rep_send, rep_recv, sum_send, sum_recv,
 ):
     units, width = wg_hbm.shape
@@ -215,13 +215,17 @@
 
     for i in (1, 8, 9):
         local[i].wait()
-    masked = (readout[...].astype(F32) * mask_ref[...].astype(F32)).astype(BF16)
     sequence = sequence_of(codes_ref[...])
     wanted = sequence * LEN + (iota((1, GROUP_TOK), 1) & (LEN - 1))
-    for start in range(0, GROUP_TOK, 256):
+
+    def unit_mask():
+        masked[...] = (readout[...].astype(F32) * mask_ref[...].astype(F32)).astype(BF16)
+
+    def unit_order(start):
         lanes = slice(start, start + 256)
         pick = (iota((GROUP_TOK, 256), 0) == wanted[:, lanes]).astype(F32).astype(BF16)
-        readout[:, lanes] = jnp.dot(masked, pick, preferred_element_type=F32).astype(BF16)
+        readout[:, lanes] = jnp.dot(masked[...], pick, preferred_element_type=F32).astype(BF16)
+
     token_score[...] = jnp.zeros_like(token_score)
     for i in (2, 3):
         local[i].wait()
@@ -234,6 +238,28 @@
             weights[rows, :], x_all[pl.ds(start, size), :], (((1,), (1,)), ((), ())),
             preferred_element_type=F32,
         )
+
+    LAST = len(CHUNKS) - 1
+    HALF = width // 2
+
+    def unit_half(weights, rows, lanes, half):
+        start, size = CHUNKS[LAST]
+        cols = pl.ds(half * HALF, HALF)
+        product = lax.dot_general(
+            weights[rows, cols], x_all[pl.ds(start, size), cols], (((1,), (1,)), ((), ())),
+            preferred_element_type=F32,
+        )
+        if half == 0:
+            both[rows, lanes] = product
+        else:
+            both[rows, lanes] += product
+
+    def last_halves(half):
+        return [
+            functools.partial(unit_half, weights, rows, pl.ds(first, CHUNKS[LAST][1]), half)
+            for weights, first in ((policy, 0), (outer, 128))
+            for rows in (gate_rows, up_rows)
+        ]
 
     def unit_policy(c):
         start, size = CHUNKS[c]
@@ -256,7 +282,7 @@
 
     def unit_reference(c):
         start, size = CHUNKS[c]
-        lanes, used = pl.ds(start, size), pl.ds(0, size)
+        lanes, used = pl.ds(start, size), pl.ds(128 if c == LAST else 0, size)
 
         def body(i, total):
             rows = pl.ds(pl.multiple_of(i * ROWS, ROWS), ROWS)
@@ -283,13 +309,21 @@
             functools.partial(unit_reference, c),
         ]
 
-    todo = []
+    todo = [unit_mask] + [functools.partial(unit_order, start) for start in range(0, GROUP_TOK, 256)]
     local[0].wait()
     left = {s: PIECES for s in RANK}
+    early = {(s, p) for s, p in ORDER[PIECES:] if p < PIECES // 2 and RANK[s] * LEN >= CHUNKS[LAST][0]}
+    early |= {(s, p) for s, p in ORDER[PIECES:] if RANK[s] * LEN < CHUNKS[LAST][0]}
+    halved = False
     for s, p in ORDER[PIECES:]:
         copies[s, p].wait_recv()
         for piece in CHILDREN.get((s, p), []):
             copies[piece].start()
+        early.discard((s, p))
+        if not early and not halved:
+            for unit in todo + last_halves(0):
+                unit()
+            todo, halved = [], True
         left[s] -= 1
         if left[s]:
             continue
@@ -307,30 +341,33 @@
                 copy.wait_recv()
             todo += reference_units(0) + reference_units(1)
         for c, (start, size) in enumerate(CHUNKS):
-            if (rank + 1) * LEN != start + size:
+            if (rank + 1) * LEN != start + size or c == LAST:
                 continue
             todo += policy_units(c)
             if c >= 2:
                 todo += reference_units(c)
-        if todo:
+        if todo and rank >= 7:
             todo.pop(0)()
-    for unit in todo:
+    for unit in todo + last_halves(1) + [functools.partial(unit_policy, LAST), functools.partial(unit_reference, LAST)]:
         unit()
 
     belongs = iota((SEQS, GROUP_TOK), 0) == sequence
     partial = jnp.sum(jnp.where(belongs, token_score[...], 0.0), axis=1, keepdims=True)
     partial = column_to_row(partial, SEQS, BLOCK)
-    near_own[...] = partial
-    near_copies = [
-        pltpu.make_async_remote_copy(
-            src_ref=near_own, dst_ref=near.at[z], send_sem=sum_send.at[d], recv_sem=sum_recv.at[z],
-            device_id=(rep, at(0, 0, d)), device_id_type=MESH,
+    own_score[...] = partial
+    offsets = [(d // 4 % 2, d % 4, d // 8) for d in range(1, SEQS)]
+    offsets.sort(key=lambda o: -(2 * o[0] + min(o[1], NY - o[1]) + min(o[2], NZ - o[2])))
+
+    def score_copy(slot, n, offset):
+        return pltpu.make_async_remote_copy(
+            src_ref=own_score, dst_ref=scores.at[slot], send_sem=sum_send.at[n], recv_sem=sum_recv.at[slot],
+            device_id=(rep, at(*offset)), device_id_type=MESH,
         )
-        for d in (4, 3, 5, 2, 6, 1, 7)
-    ]
-    for copy in near_copies:
+
+    score_copies = [score_copy(me, n, offset) for n, offset in enumerate(offsets)]
+    for copy in score_copies:
         copy.start()
-    near[z] = partial
+    scores[me] = partial
 
     for copy in slab_copies:
         copy.wait_recv()
@@ -352,48 +389,17 @@
             average[rows, lanes] = total * 0.25
         return 0
 
-    half = units // STEP // 2
-    lax.fori_loop(0, half, pseudo, 0)
-
-    for d in range(1, NZ):
-        pltpu.make_async_remote_copy(
-            src_ref=near_own, dst_ref=near.at[(z + d) % 8], send_sem=sum_send.at[d],
-            recv_sem=sum_recv.at[(z + d) % 8], device_id=(rep, at(0, 0, d)), device_id_type=MESH,
-        ).wait_recv()
-    partial = near[0]
-    for i in range(1, NZ):
-        partial = partial + near[i]
-    plane = x * 4 + y
-    wide_own[...] = partial
-    wide_copies = [
-        pltpu.make_async_remote_copy(
-            src_ref=wide_own, dst_ref=wide.at[plane], send_sem=sum_send.at[8 + d],
-            recv_sem=sum_recv.at[8 + plane], device_id=(rep, at(d // 4, d % 4, 0)), device_id_type=MESH,
-        )
-        for d in (6, 5, 7, 2, 4, 1, 3)
-    ]
-    for copy in wide_copies:
-        copy.start()
-    wide[plane] = partial
-
-    lax.fori_loop(half, units // STEP, pseudo, 0)
-
-    for d in range(1, NX * NY):
-        other = ((x + d // 4) % 2) * 4 + (y + d % 4) % 4
-        pltpu.make_async_remote_copy(
-            src_ref=wide_own, dst_ref=wide.at[other], send_sem=sum_send.at[8 + d],
-            recv_sem=sum_recv.at[8 + other], device_id=(rep, at(d // 4, d % 4, 0)), device_id_type=MESH,
-        ).wait_recv()
-    partial = wide[0]
-    for i in range(1, NX * NY):
-        partial = partial + wide[i]
-    relative_out[...] = partial
+    lax.fori_loop(0, units // STEP, pseudo, 0)
 
     for piece in ORDER[PIECES:]:
         copies[piece].wait_send()
     for copy in (gate_far, up_far, gate_near, up_near, gate_pass, up_pass, *slab_copies):
         copy.wait_send()
-    for copy in near_copies + wide_copies:
+    for n, offset in enumerate(offsets):
+        score_copy(at(*offset), n, offset).wait_recv()
+    relative_out[...] = jnp.sum(scores[...], axis=0)
+
+    for copy in score_copies:
         copy.wait_send()
 
 
@@ -420,19 +426,18 @@
             pltpu.VMEM((units, part), BF16),
             pltpu.VMEM((4, units, part), BF16),
             pltpu.VMEM((units, GROUP_TOK), BF16),
+            pltpu.VMEM((units, GROUP_TOK), BF16),
             pltpu.VMEM((2 * units, 256), F32),
             pltpu.VMEM((1, GROUP_TOK), F32),
-            pltpu.VMEM((NZ, 1, BLOCK), F32),
-            pltpu.VMEM((NX * NY, 1, BLOCK), F32),
-            pltpu.VMEM((1, BLOCK), F32),
+            pltpu.VMEM((SEQS, 1, BLOCK), F32),
             pltpu.VMEM((1, BLOCK), F32),
             pltpu.SemaphoreType.DMA((10,)),
             pltpu.SemaphoreType.DMA((SEQS * PIECES,)),
             pltpu.SemaphoreType.DMA((SEQS * PIECES,)),
             pltpu.SemaphoreType.DMA((9,)),
             pltpu.SemaphoreType.DMA((9,)),
-            pltpu.SemaphoreType.DMA((16,)),
-            pltpu.SemaphoreType.DMA((16,)),
+            pltpu.SemaphoreType.DMA((SEQS,)),
+            pltpu.SemaphoreType.DMA((SEQS,)),
         ],
         compiler_params=pltpu.CompilerParams(
             collective_id=0, has_side_effects=True, vmem_limit_bytes=K1_LIMIT

time: 80.6 us -> 79.2 us (0.983); the launches traced: 80.4 us -> 78.2 us
  Pallas kernels: 79.5 us -> 77.3 us
    pallas_call x1, Pallas kernels: 73 us -> 70.8 us  [gather_forward(): pl.pallas_call(gather_kernel, name='gather_forward', out_shape=(jax.Shape...]
where the time goes in v5:
time: 79.2 us; the launch traced here: 78.2 us
  Pallas kernels  77.3 us (98%)
  between operations  0.87 us (1%)
    pallas_call x1, Pallas kernels, gather_forward(): pl.pallas_call(gather_kernel, name='gather_forward', out_shape=(jax.Shape...  70.8 us
    pallas_call x1, Pallas kernels, backward(): pl.pallas_call(backward_kernel, name='backward', out_shape=(jax.ShapeDtyp...  6.46 us

profile of v5, /device:TPU:2, one launch (start us, length us, event | category | flops | bytes accessed | tf_op | source)
XLA Modules:
  0.0 78.2 jit_solution(15027039181944616218)
XLA Ops:
  0.6 0.0 copy-start
  0.6 0.0 copy-start.1
  0.7 0.0 copy-start.2
  0.7 0.0 copy-start.3
  0.7 70.8 %gather_forward.1 = (bf16[1024,4096]{1,0:T(8,128)(2,1)S(1)}, f32[448,1024]{1,0:T(8,128)S(1)}, f32[224,1024]{1,0:T(8,128)S(1)}, f32[1,128]{1,0:T(1,128)S(1)}) custom-call(s32[1,1024]{1,0:T(1,128)} %constant.2.clone.codes_hbm.codes_ref, s32[1,1024]{1,0:T(1,128)} %bitcast.7, bf16[16,4096]{1,0:T(8,128)(2,1)} %tokens_hbm.1, bf16[224,1024]{1,0:T(8,128)(2,1)} %bitcast.6, ...), custom_call_target="tpu_custom_call" | custom-call | tf_op jit(solution)/shard_map/gather_forward/pallas_call | solution.py:410
  71.5 0.0 copy-done
  71.5 0.0 copy-done.1
  71.5 0.0 copy-done.2
  71.5 0.0 copy-done.3
  71.5 6.5 %backward.1 = (f32[1]{0:T(128)}, bf16[1,224,4096]{2,1,0:T(8,128)(2,1)}, bf16[1,224,4096]{2,1,0:T(8,128)(2,1)}, bf16[224,1024]{1,0:T(8,128)(2,1)}, f32[224,1024]{1,0:T(8,128)}) custom-call(s32[1,1024]{1,0:T(1,128)S(1)} %copy-done.2, s32[1,64]{1,0:T(1,128)S(1)} %copy-done.3, f32[1,128]{1,0:T(1,128)S(1)} %get-tuple-element.9.relative_ref, ...), custom_call_target="tpu_custom_call" | custom-call | tf_op jit(solution)/shard_map/backward/pallas_call | solution.py:514
Async XLA Ops:
  0.6 70.9 %copy-start = (bf16[224,1024]{1,0:T(8,128)(2,1)S(1)}, bf16[224,1024]{1,0:T(8,128)(2,1)}, u32[]{:S(2)}) copy-start(bf16[224,1024]{1,0:T(8,128)(2,1)} %outer.1) | copy-start | bytes 1376260
  0.6 70.9 %copy-start.1 = (f32[224,1024]{1,0:T(8,128)S(1)}, f32[224,1024]{1,0:T(8,128)}, u32[]{:S(2)}) copy-start(f32[224,1024]{1,0:T(8,128)} %moment.1) | copy-start | bytes 2752516
  0.7 70.9 %copy-start.2 = (s32[1,1024]{1,0:T(1,128)S(1)}, s32[1,1024]{1,0:T(1,128)}, u32[]{:S(2)}) copy-start(s32[1,1024]{1,0:T(1,128)} %constant.2.clone.codes_hbm.codes_ref) | copy-start | bytes 12292
  0.7 70.9 %copy-start.3 = (s32[1,64]{1,0:T(1,128)S(1)}, s32[1,64]{1,0:T(1,128)}, u32[]{:S(2)}) copy-start(s32[1,64]{1,0:T(1,128)} %order_ref.1) | copy-start | bytes 772
